TPU v7x, 768 devices: a whole 4x8x12 slice. The times are simulated.
768 devices in a mesh: space: 64 (over z_hi, y, core), band: 12 (over x, z_lo).
Axes of the slice: x: 4, y: 8, z: 12 (z_hi: 4, z_lo: 3; z = z_hi * 3 + z_lo), core: 2. Of those that a mesh axis runs over, the one named last changes fastest.
Arguments:
- psi: float32 [192, 263424], P('band', 'space'), may hold values from -400 to 400
- ham: bfloat16 [768, 512, 512], P('space'), may hold values from -2 to 2, as said below
- conn: int32 [768, 512], P('space'), may hold values from 0 to 4703, as said below
- face_rows: int32 [37632], P('space'), may hold values from 0 to 4115, as said below
Outputs:
- ortho: float32 [192, 263424], P('band', 'space')
Inputs may be any that keep to these rules, and one draw needn't show every extreme that they name: `conn`: rows s * 12 to (s + 1) * 12 - 1 are the elements of domain s. Entries at element-local nodes below 448 name the domain's own rows 0 to 4115; entries at and above 448 name ghost slots 4116 + j, where ghost slot j is the node listed at position j of face_rows of domain (s + 1) mod 64. Every own row and every ghost slot of a domain is named by some element. `face_rows`: entries s * 588 to (s + 1) * 588 - 1 are 588 distinct own rows of domain s: the nodes of its lower face. `ham`: each matrix is symmetric.
All inputs are finite; a program needn't handle non-finite values.
Results may differ from a plain program's by a relative error of at most 0.0037.
Values may be sent and summed in bfloat16 or wider, within the bound.
A program may use at most 32 MiB of HBM per device.

v0:
```python
import jax
import jax.numpy as jnp
from jax import lax
from jax.sharding import PartitionSpec as P

NODE_EL = 512


CENTER = 6.25
HALF_WIDTH = 7.5


def from_behind(block, axis, distance):
    devices = range(lax.axis_size(axis))
    route = [((i - distance) % len(devices), i) for i in devices]
    return lax.ppermute(block, axis, route)


def per_device(psi, ham, conn, face_rows):
    band_count, node_count = psi.shape
    elem_count = conn.shape[0]
    face_count = face_rows.shape[0]
    flat_conn = conn.reshape(-1)

    def apply_operator(field):
        rounded = field.astype(jnp.bfloat16)
        face_values = jnp.take(rounded, face_rows, axis=1)
        ghost = from_behind(face_values, "space", -1)
        extended = jnp.concatenate([rounded, ghost], axis=1)
        gathered = jnp.take(extended, flat_conn, axis=1).reshape(band_count, elem_count, NODE_EL)
        products = jnp.einsum("bem,eml->bel", gathered, ham, preferred_element_type=jnp.float32)
        summed = jnp.zeros((band_count, node_count + face_count), jnp.float32)
        summed = summed.at[:, flat_conn].add(products.reshape(band_count, elem_count * NODE_EL))
        upper_sums = summed[:, node_count:]
        owned = summed[:, :node_count]
        received = from_behind(upper_sums, "space", 1)
        return owned.at[:, face_rows].add(received)

    current = (apply_operator(psi) - CENTER * psi) / HALF_WIDTH
    scaled = (apply_operator(current) - CENTER * current) / HALF_WIDTH
    following = 2.0 * scaled - psi
    node_rows = lax.all_to_all(following, "band", split_axis=1, concat_axis=0, tiled=True)
    partial_value = lax.dot_general(
        node_rows,
        node_rows,
        (((1,), (1,)), ((), ())),
        precision=lax.Precision.HIGHEST,
        preferred_element_type=jnp.float32,
    )
    correlation = lax.psum(partial_value, ("space", "band"))
    correlation = correlation / (node_count * lax.axis_size("space"))
    factor = jnp.linalg.cholesky(correlation)
    orthonormal = jax.scipy.linalg.solve_triangular(factor, node_rows, lower=True)
    return lax.all_to_all(orthonormal, "band", split_axis=0, concat_axis=1, tiled=True)


def solution(mesh):
    placed = (P("band", "space"), P("space", None, None), P("space", None), P("space"))
    return jax.shard_map(
        per_device, mesh=mesh, in_specs=placed, out_specs=P("band", "space"), check_vma=False
    )
```

profile of v0, /device:TPU:6, one launch (start us, length us, event | category | flops | bytes accessed | tf_op | source)
XLA Modules:
  0.0 763.4 jit_solution(3395213916208499668)
XLA Ops:
  6.5 0.7 compare_select_fusion.2
  7.2 0.7 compare_and_fusion.1
  7.9 1.4 copy.74
  9.4 2.0 gather_fusion
  11.5 16.9 %collective-permute-start = (bf16[16,588]{0,1:T(8,128)(2,1)S(1)}, bf16[16,588]{0,1:T(8,128)(2,1)S(1)}, u32[]{:S(2)}, u32[]{:S(2)}) collective-permute-start(bf16[16,588]{0,1:T(8,128)(2,1)S(1)} %select_bitcast_fusion), channel_id=1, source_target_pairs={{12,0},{24,12},{36,24},{48,36},{60,48},{72,60},{84,72},{96,84},{10... | collective-permute-start | bytes 56456 | tf_op jit(solution)/shard_map/ppermute | solution.py:16
  28.4 0.8 reshape.87
  29.2 0.8 copy.98
  30.0 4.3 collective-permute-done
  34.6 22.1 %gather_fusion.1 = bf16[6144,16]{1,0:T(8,128)(2,1)} fusion(bf16[16,4704]{0,1:T(8,128)(2,1)S(1)} %pad_maximum_fusion, s32[6144]{0:T(1024)S(1)} %fusion.16), kind=kCustom, calls=%fused_computation.1.clone | custom fusion | bytes 417792 | tf_op jit(solution)/shard_map/jit(_take)/gather | solution.py:30
  56.7 4.4 broadcast_select_fusion
  61.1 3.8 convolution_bitcast_fusion.1
  64.9 2.2 copy.77
  67.1 34.1 %scatter_custom_fusion = f32[16,4704]{0,1:T(8,128)S(1)} fusion(s32[6144]{0:T(1024)S(1)} %bitcast.85, f32[6144,16]{1,0:T(8,128)} %copy.77, f32[]{:T(128)} %constant.116.clone.1), kind=kCustom, calls=%fused_computation.13 | custom fusion | flops 98304 | bytes 301568 | tf_op jit(solution)/shard_map/scatter-add | solution.py:33
  101.2 1.9 collective-permute-start.1
  103.1 1.5 slice.93
  104.6 10.2 %collective-permute-done.1 = f32[16,588]{0,1:T(8,128)S(1)} collective-permute-done((f32[16,588]{0,1:T(8,128)S(1)}, f32[16,588]{0,1:T(8,128)S(1)}, u32[]{:S(2)}, u32[]{:S(2)}) %collective-permute-start.1) | collective-permute-done | bytes 37664 | tf_op jit(solution)/shard_map/ppermute | solution.py:16
  114.8 9.1 %scatter_custom_fusion.1 = f32[16,4116]{0,1:T(8,128)} fusion(f32[16,4116]{0,1:T(8,128)} %slice.93, s32[588]{0:T(1024)S(1)} %compare_select_fusion.2, f32[16,588]{0,1:T(8,128)S(1)} %collective-permute-done.1), kind=kCustom, calls=%fused_computation.22 | custom fusion | flops 9408 | bytes 566528 | tf_op jit(solution)/shard_map/scatter-add | solution.py:37
  123.9 2.2 copy.78
  126.6 2.0 gather_fusion.2
  128.7 2.1 collective-permute-start.2
  130.8 1.3 collective-permute-done.2
  132.2 0.6 copy.81
  132.7 22.1 %gather_fusion.3 = bf16[6144,16]{1,0:T(8,128)(2,1)} fusion(bf16[16,4704]{0,1:T(8,128)(2,1)S(1)} %copy.81, s32[6144]{0:T(1024)S(1)} %fusion.16), kind=kCustom, calls=%fused_computation.3.clone | custom fusion | bytes 417792 | tf_op jit(solution)/shard_map/jit(_take)/gather | solution.py:30
  154.8 4.4 broadcast_select_fusion.1
  159.2 3.8 convolution_bitcast_fusion
  163.0 2.2 copy.84
  165.2 34.1 %scatter_custom_fusion.2 = f32[16,4704]{0,1:T(8,128)S(1)} fusion(s32[6144]{0:T(1024)S(1)} %bitcast.86, f32[6144,16]{1,0:T(8,128)} %copy.84, f32[]{:T(128)} %constant.116.clone.1), kind=kCustom, calls=%fused_computation.11 | custom fusion | flops 98304 | bytes 301568 | tf_op jit(solution)/shard_map/scatter-add | solution.py:33
  199.3 1.9 collective-permute-start.3
  201.2 1.5 slice.95
  202.7 9.9 %collective-permute-done.3 = f32[16,588]{0,1:T(8,128)S(1)} collective-permute-done((f32[16,588]{0,1:T(8,128)S(1)}, f32[16,588]{0,1:T(8,128)S(1)}, u32[]{:S(2)}, u32[]{:S(2)}) %collective-permute-start.3) | collective-permute-done | bytes 37664 | tf_op jit(solution)/shard_map/ppermute | solution.py:16
  212.7 9.1 %scatter_custom_fusion.3 = f32[16,4116]{0,1:T(8,128)} fusion(f32[16,4116]{0,1:T(8,128)} %slice.95, s32[588]{0:T(1024)S(1)} %compare_select_fusion.2, f32[16,588]{0,1:T(8,128)S(1)} %collective-permute-done.3), kind=kCustom, calls=%fused_computation.20 | custom fusion | flops 9408 | bytes 566528 | tf_op jit(solution)/shard_map/scatter-add | solution.py:37
  221.7 2.2 copy.85
  224.2 0.8 copy.86
  225.0 13.0 %all-to-all-start = ((f32[16,12,343]{2,0,1:T(8,128)}), f32[16,12,343]{2,0,1:T(8,128)S(1)}, u32[]{:S(2)}, u32[]{:S(2)}) async-start(f32[16,12,343]{2,0,1:T(8,128)} %copy.86), calls=%async_computation | async-start | bytes 589824 | tf_op jit(solution)/shard_map/all_to_all | solution.py:42
  238.0 6.8 all-to-all-done
  244.9 1.2 fusion.17
  246.1 442.8 %all-reduce.5.cloned.1.call-done = f32[192,192]{0,1:T(8,128)} async-done(((f32[192,192]{0,1:T(8,128)}), f32[192,192]{0,1:T(8,128)}) %all-reduce.5.cloned.1.call-update) | async-done | bytes 147472 | tf_op jit(solution)/shard_map/psum | solution.py:50
  688.9 0.9 broadcast_multiply_fusion
  690.0 1.0 fusion.8
  691.0 11.7 %cholesky.51 = f32[128,128]{1,0:T(8,128)S(1)} custom-call(f32[128,128]{1,0:T(8,128)S(1)} %cholesky.124), custom_call_target="Cholesky" | custom-call | tf_op jit(solution)/shard_map/jit(cholesky)/cholesky | solution.py:52
  702.7 9.8 %custom-call.15 = f32[1,128,128]{1,2,0:T(8,128)S(1)} custom-call(f32[1,128,128]{2,1,0:T(8,128)S(1)} %get-tuple-element.28), custom_call_target="InvertDiagBlocksLowerTriangular" | custom-call | tf_op jit(solution)/shard_map/jit(cholesky)/cholesky | solution.py:52
  712.9 5.8 cholesky.110
  718.8 0.7 compare_reduce_fusion
  719.5 0.6 compare_reduce_fusion.1
  721.7 19.7 %custom-call.16 = f32[2,128,128]{1,2,0:T(8,128)S(1)} custom-call(f32[2,128,128]{2,1,0:T(8,128)S(1)} %pad_maximum_fusion.3), custom_call_target="InvertDiagBlocksLowerTriangular" | custom-call | tf_op jit(solution)/shard_map/jit(_solve_triangular)/triangular_solve | solution.py:53
  741.3 0.5 fusion.9
  742.9 12.7 %all_to_all.38 = f32[12,16,343]{2,1,0:T(8,128)S(1)} all-to-all(f32[12,16,343]{2,1,0:T(8,128)S(1)} %bitcast.79), channel_id=1, replica_groups=mesh['space'=64,'band'=12] {'band'}, dimensions={0} | all-to-all | bytes 526848 | tf_op jit(solution)/shard_map/all_to_all | solution.py:54
  755.6 0.9 all_to_all.35
  (41 shorter events, 3.5 us)
Async XLA Ops:
  11.5 22.9 %collective-permute-start = (bf16[16,588]{0,1:T(8,128)(2,1)S(1)}, bf16[16,588]{0,1:T(8,128)(2,1)S(1)}, u32[]{:S(2)}, u32[]{:S(2)}) collective-permute-start(bf16[16,588]{0,1:T(8,128)(2,1)S(1)} %select_bitcast_fusion), channel_id=1, source_target_pairs={{12,0},{24,12},{36,24},{48,36},{60,48},{72,60},{84,72},{96,84},{10... | collective-permute-start | bytes 56456 | tf_op jit(solution)/shard_map/ppermute | solution.py:16
  101.2 13.6 %collective-permute-start.1 = (f32[16,588]{0,1:T(8,128)S(1)}, f32[16,588]{0,1:T(8,128)S(1)}, u32[]{:S(2)}, u32[]{:S(2)}) collective-permute-start(f32[16,588]{0,1:T(8,128)S(1)} %slice.94), channel_id=1, source_target_pairs={{756,0},{0,12},{12,24},{24,36},{36,48},{48,60},{60,72},{72,84},{84... | collective-permute-start | bytes 112904 | tf_op jit(solution)/shard_map/ppermute | solution.py:16
  104.6 21.4 %copy-start = (f32[16,4116]{1,0:T(8,128)S(1)}, f32[16,4116]{1,0:T(8,128)}, u32[]{:S(2)}) copy-start(f32[16,4116]{1,0:T(8,128)} %param.8) | copy-start | bytes 790276
  128.7 3.4 collective-permute-start.2
  199.3 13.4 %collective-permute-start.3 = (f32[16,588]{0,1:T(8,128)S(1)}, f32[16,588]{0,1:T(8,128)S(1)}, u32[]{:S(2)}, u32[]{:S(2)}) collective-permute-start(f32[16,588]{0,1:T(8,128)S(1)} %slice.96), channel_id=1, source_target_pairs={{756,0},{0,12},{12,24},{24,36},{36,48},{48,60},{60,72},{72,84},{84... | collective-permute-start | bytes 112904 | tf_op jit(solution)/shard_map/ppermute | solution.py:16
  225.0 19.8 %all-to-all-start = ((f32[16,12,343]{2,0,1:T(8,128)}), f32[16,12,343]{2,0,1:T(8,128)S(1)}, u32[]{:S(2)}, u32[]{:S(2)}) async-start(f32[16,12,343]{2,0,1:T(8,128)} %copy.86), calls=%async_computation | async-start | bytes 589824 | tf_op jit(solution)/shard_map/all_to_all | solution.py:42
  238.0 450.9 %all-reduce.5.cloned.1.call-start = ((), (), s32[]{:S(2)}) async-start(), calls=%async_computation.2 | async-start | bytes 393216 | tf_op jit(solution)/shard_map/psum | solution.py:50
Sparse Core Ops, SparseCore 0:
  246.2 442.6 all-reduce.4
where the time goes:
time: 767 us; the launch traced here: 763 us
  waiting for transfers between devices  475 us (62%)
  other arithmetic  148 us (19%)
  local copies, waits for them, and re-layouts  66.3 us (9%)
  starting transfers between devices  35.8 us (5%)
  between operations  15.1 us (2%)
  blocking collectives  12.7 us (2%)
  matrix products  10.5 us (1%)
    psum x1, waiting for transfers between devices, per_device(): correlation = lax.psum(partial_value, ('space', 'band'))  443 us
    scatter-add x2, other arithmetic, apply_operator(): summed.at[:, flat_conn]  68.1 us
    gather x2, local copies, waits for them, and re-layouts, apply_operator(): jnp.take(extended, flat_conn, axis=1)  44.1 us
    another operation x7, other arithmetic, per_device(): factor = jnp.linalg.cholesky(correlation)  28.8 us
    ppermute x4, waiting for transfers between devices, from_behind(): return lax.ppermute(block, axis, route)  25.7 us
    ppermute x4, starting transfers between devices, from_behind(): return lax.ppermute(block, axis, route)  22.9 us
    another operation x7, other arithmetic, per_device(): jax.scipy.linalg.solve_triangular(factor, node_rows, lower=True)  19.8 us
    scatter-add x2, other arithmetic, apply_operator(): return owned.at[:, face_rows].add(received)  18.1 us
  transfers between devices with their start and end apart: 6, of which 6 were waited for; matrix products, arithmetic and copies ran while one was open for 1% of the time, Pallas kernels for 0%

commit v1 on v0

v1 whole, which is shorter than its diff:
```python
import functools

import jax
import jax.numpy as jnp
from jax import lax
from jax.experimental import pallas as pl
from jax.experimental.pallas import tpu as pltpu
from jax.sharding import PartitionSpec as P

NODE_EL = 512
OWN_EL = 448
CENTER = 6.25
HALF_WIDTH = 7.5
LO = 256
MESH = pl.DeviceIdType.MESH
BF = jnp.bfloat16
F32 = jnp.float32
VMEM_LIMIT = 60 * 1024 * 1024

CORES, YS, ZS = 2, 8, 4
NT = (((1,), (1,)), ((), ()))
TN = (((0,), (0,)), ((), ()))


def nn(a, b):
    return jnp.dot(a, b, preferred_element_type=F32)


def nt(a, b):
    return lax.dot_general(a, b, NT, preferred_element_type=F32)


def remote(src, dst, send, recv, where):
    return pltpu.make_async_remote_copy(
        src_ref=src, dst_ref=dst, send_sem=send, recv_sem=recv, device_id=where, device_id_type=MESH
    )


def split(value):
    high = value.astype(BF)
    return high, (value - high.astype(F32)).astype(BF)


def filter_kernel(
    psi_ref, ham_ref, conn_ref, face_ref, out_ref,
    onehot, onehot_face, hi_ref, hi_face, base, field, sums, xb, xg, gathered, products,
    send1, send2, send3, send4, got1, got2, got3, got4, send_sem, recv_sem,
):
    bands, nodes = psi_ref.shape
    elems = conn_ref.shape[0]
    faces = face_ref.shape[1]
    own_blocks = pl.cdiv(nodes, LO)
    ghost_blocks = pl.cdiv(faces, LO)
    face_pad = got1.shape[1]
    shift = own_blocks * LO - nodes
    domains = lax.axis_size("space")
    me = lax.axis_index("space")
    below = {"space": lax.rem(me + domains - 1, domains)}
    above = {"space": lax.rem(me + 1, domains)}

    barrier = pltpu.get_barrier_semaphore()
    for there in (below, above):
        pl.semaphore_signal(barrier, inc=1, device_id=there, device_id_type=MESH)

    for h in range(own_blocks):
        rows = slice(h * bands, (h + 1) * bands)
        if (h + 1) * LO <= nodes:
            value = psi_ref[:, h * LO:(h + 1) * LO]
            base[rows, :] = value
            xb[rows, :] = value.astype(BF)
        else:
            base[rows, :] = jnp.zeros((bands, LO), F32)
            base[rows, 0:nodes - h * LO] = psi_ref[:, h * LO:nodes]
            xb[rows, :] = base[rows, :].astype(BF)

    hi_face[...] = jnp.full(hi_face.shape, -1, jnp.int32)
    hi_face[:, 0:faces] = jnp.broadcast_to(face_ref[...], (bands, faces))
    named = hi_face[...]
    lanes = lax.broadcasted_iota(jnp.int32, (LO, face_pad), 0)
    onehot_face[...] = jnp.where(lanes == (named[0:1, :] & (LO - 1)), 1.0, 0.0).astype(BF)
    hi_face[...] = named >> 8

    def take_face(blocks):
        table = nn(blocks, onehot_face[...])
        which = hi_face[...]
        total = jnp.zeros((bands, face_pad), F32)
        for h in range(own_blocks):
            total = jnp.where(which == h, table[h * bands:(h + 1) * bands, :], total)
        return total

    send1[...] = take_face(xb[...]).astype(BF)
    pl.semaphore_wait(barrier, 2)
    copy1 = remote(send1, got1, send_sem.at[0], recv_sem.at[0], below)
    copy1.start()

    spot = lax.broadcasted_iota(jnp.int32, (1, NODE_EL), 1)
    depth = lax.broadcasted_iota(jnp.int32, (LO, NODE_EL), 0)

    def prepare(e, carry):
        cols = pl.ds(pl.multiple_of(e * NODE_EL, NODE_EL), NODE_EL)
        named = conn_ref[pl.ds(e, 1), :]
        named = jnp.where(spot >= OWN_EL, named + shift, named)
        onehot[:, cols] = jnp.where(depth == (named & (LO - 1)), 1.0, 0.0).astype(BF)
        hi_ref[:, cols] = jnp.broadcast_to(named >> 8, (bands, NODE_EL))
        return carry

    lax.fori_loop(0, elems, prepare, 0)

    def gather_own(e, carry):
        cols = pl.ds(pl.multiple_of(e * NODE_EL, NODE_EL), NODE_EL)
        table = nn(xb[...], onehot[:, cols])
        which = hi_ref[:, cols]
        total = jnp.zeros((bands, NODE_EL), F32)
        for h in range(own_blocks):
            total = jnp.where(which == h, table[h * bands:(h + 1) * bands, :], total)
        gathered[:, cols] = total.astype(BF)
        return carry

    def multiply(e, carry):
        cols = pl.ds(pl.multiple_of(e * NODE_EL, NODE_EL), NODE_EL)
        tail = pl.ds(pl.multiple_of(e * NODE_EL + NODE_EL - 128, 128), 128)
        table = nn(xg[...], onehot[:, tail])
        which = hi_ref[:, tail]
        total = gathered[:, tail].astype(F32)
        for h in range(ghost_blocks):
            total = jnp.where(which == own_blocks + h, table[h * bands:(h + 1) * bands, :], total)
        gathered[:, tail] = total.astype(BF)
        products[:, cols] = nn(gathered[:, cols], ham_ref[e])
        return carry

    def scatter_all(e, carry):
        cols = pl.ds(pl.multiple_of(e * NODE_EL, NODE_EL), NODE_EL)
        high, low = split(products[:, cols])
        which = hi_ref[:, cols]
        zero = jnp.zeros_like(high)
        keep = [which == h for h in range(own_blocks + ghost_blocks)]
        left = jnp.concatenate([jnp.where(k, high, zero) for k in keep], axis=0)
        right = jnp.concatenate([jnp.where(k, low, zero) for k in keep], axis=0)
        sums[...] += nt(left, onehot[:, cols]) + nt(right, onehot[:, cols])
        return carry

    def put_face(received):
        high, low = split(received)
        which = hi_face[...]
        zero = jnp.zeros_like(high)
        keep = [which == h for h in range(own_blocks)]
        left = jnp.concatenate([jnp.where(k, high, zero) for k in keep], axis=0)
        right = jnp.concatenate([jnp.where(k, low, zero) for k in keep], axis=0)
        return nt(left, onehot_face[...]) + nt(right, onehot_face[...])

    def put_ghost(values):
        for h in range(ghost_blocks):
            width = min(LO, face_pad - h * LO)
            xg[h * bands:(h + 1) * bands, 0:width] = values[:, h * LO:h * LO + width].astype(BF)

    own = slice(0, own_blocks * bands)

    def upper():
        parts = []
        for h in range(ghost_blocks):
            width = min(LO, face_pad - h * LO)
            start = (own_blocks + h) * bands
            parts.append(sums[start:start + bands, 0:width])
        return jnp.concatenate(parts, axis=1)

    xg[...] = jnp.zeros(xg.shape, BF)
    lax.fori_loop(0, elems, gather_own, 0)
    copy1.wait()
    put_ghost(got1[...])
    sums[...] = jnp.zeros(sums.shape, F32)
    lax.fori_loop(0, elems, multiply, 0)
    lax.fori_loop(0, elems, scatter_all, 0)

    send2[...] = upper()
    copy2 = remote(send2, got2, send_sem.at[1], recv_sem.at[1], above)
    copy2.start()
    partial_value = (sums[own, :] - CENTER * base[...]) / HALF_WIDTH
    field[...] = partial_value
    high, low = split(partial_value)
    send3[...] = take_face(high) + take_face(low)
    copy3 = remote(send3, got3, send_sem.at[2], recv_sem.at[2], below)
    copy3.start()
    copy2.wait()
    field[...] += put_face(got2[...] / HALF_WIDTH)
    xb[...] = field[...].astype(BF)
    lax.fori_loop(0, elems, gather_own, 0)
    copy3.wait()
    put_ghost(got3[...] + send2[...] / HALF_WIDTH)
    sums[...] = jnp.zeros(sums.shape, F32)
    lax.fori_loop(0, elems, multiply, 0)
    lax.fori_loop(0, elems, scatter_all, 0)

    send4[...] = upper()
    copy4 = remote(send4, got4, send_sem.at[3], recv_sem.at[3], above)
    copy4.start()
    partial_value = sums[own, :] - CENTER * field[...]
    copy4.wait()
    field[...] = 2.0 * ((partial_value + put_face(got4[...])) / HALF_WIDTH) - base[...]

    groups, _, width = out_ref.shape
    per = width // 128
    for piece in range(groups * per):
        dst = slice((piece % per) * 128, (piece % per + 1) * 128)
        if piece // 2 < own_blocks:
            rows = slice(piece // 2 * bands, (piece // 2 + 1) * bands)
            src = slice((piece % 2) * 128, (piece % 2 + 1) * 128)
            out_ref[piece // per, :, dst] = field[rows, src].astype(BF)
        else:
            out_ref[piece // per, :, dst] = jnp.zeros((bands, 128), BF)


def factor_inverse(mat):
    size, wide = mat.shape
    step = 8
    lane = lax.broadcasted_iota(jnp.int32, (step, 128), 1)
    sub = lax.broadcasted_iota(jnp.int32, (step, 128), 0)
    halves = wide // 128
    for start in range(0, size, step):
        tile, at = start // 128, start % 128
        block = [mat[start:start + step, t * 128:(t + 1) * 128] for t in range(halves)]
        head = block[tile]
        d = {}
        for j in range(step):
            column = jnp.broadcast_to(head[:, at + j:at + j + 1], (step, 128))
            for i in range(j, step):
                d[i, j] = jnp.broadcast_to(column[i:i + 1, :], (step, 128))
        inverse = []
        factor = {}
        for k in range(step):
            scale = lax.rsqrt(d[k, k])
            inverse.append(scale)
            for i in range(k + 1, step):
                factor[i, k] = d[i, k] * scale
            for i in range(k + 1, step):
                for m in range(k + 1, i + 1):
                    d[i, m] = d[i, m] - factor[i, k] * factor[m, k]
        inside = (lane >= at) & (lane < at + step)
        fresh = []
        for t in range(halves):
            rows = []
            result = jnp.zeros((step, 128), F32)
            for i in range(step):
                row = jnp.broadcast_to(block[t][i:i + 1, :], (step, 128))
                if t == tile:
                    row = jnp.where(inside, jnp.where(lane == at + i, 1.0, 0.0), row)
                for j in range(i):
                    row = row - factor[i, j] * rows[j]
                row = row * inverse[i]
                rows.append(row)
                result = jnp.where(sub == i, row, result)
            fresh.append(result)
        fresh = jnp.concatenate(fresh, axis=1)
        mat[start:start + step, :] = fresh
        if start + step < size:
            first = (start + step) // 128 * 128
            update = lax.dot_general(
                fresh[:, first:], fresh, TN, precision=lax.Precision.HIGHEST, preferred_element_type=F32
            )
            rest = mat[start + step:size, :]
            column = lax.broadcasted_iota(jnp.int32, rest.shape, 1)
            rest = jnp.where((column >= start) & (column < start + step), 0.0, rest)
            mat[start + step:size, :] = rest - update[start + step - first:size - first, :]


def tail_kernel(
    total_nodes, in_ref, out_ref,
    rows_all, gram, half_in, half, band_in, y_in, z_in, whole, mat, ortho, back,
    a_send, a_recv, c_send, c_recv, r_send, r_recv, y_send, y_recv, z_send, z_recv,
    g_send, g_recv, b_send, b_recv,
):
    groups, bands, width = in_ref.shape
    count = groups * bands
    wide = gram.shape[1]
    band = lax.axis_index("band")
    space = lax.axis_index("space")
    core = lax.rem(space, CORES)
    y = lax.rem(space // CORES, YS)
    z = space // (CORES * YS)

    def band_peer(d):
        return {"band": lax.rem(band + d, groups)}

    def y_peer(d):
        return {"space": (z * YS + lax.rem(y + d, YS)) * CORES + core}

    def z_peer(d):
        return {"space": (lax.rem(z + d, ZS) * YS + y) * CORES + core}

    twin = {"space": space + 1 - 2 * core}
    peers = [band_peer(d) for d in range(1, groups)]
    peers += [y_peer(d) for d in range(1, YS)]
    peers += [z_peer(d) for d in range(1, ZS)]
    peers.append(twin)
    barrier = pltpu.get_barrier_semaphore()
    for there in peers:
        pl.semaphore_signal(barrier, inc=1, device_id=there, device_id_type=MESH)
    rows_all[count:, :] = jnp.zeros((rows_all.shape[0] - count, width), BF)
    pl.semaphore_wait(barrier, len(peers))

    def finish(copies):
        for c in copies:
            c.wait()

    mine = pl.ds(pl.multiple_of(band * bands, bands), bands)
    copies = []
    for d in range(1, groups):
        there = band_peer(d)
        copies.append(remote(in_ref.at[there["band"]], rows_all.at[mine], a_send.at[d - 1], a_recv.at[d - 1], there))
        copies[-1].start()
    rows_all[mine, :] = in_ref[band]
    finish(copies)

    local = nt(rows_all[0:count, :], rows_all[...])
    gram[...] = local
    part = count // CORES
    theirs = pl.ds(pl.multiple_of((1 - core) * part, 8), part)
    ours = pl.ds(pl.multiple_of(core * part, 8), part)
    copy = remote(gram.at[theirs], half_in, c_send.at[0], c_recv.at[0], twin)
    copy.start()
    copy.wait()
    half[...] = (gram[ours, :] + half_in[...]).reshape(half.shape)

    copies = []
    for d in range(1, groups):
        there = band_peer(d)
        copies.append(remote(half.at[there["band"]], band_in.at[d - 1], r_send.at[d - 1], r_recv.at[d - 1], there))
        copies[-1].start()
    finish(copies)
    value = half[band]
    for d in range(1, groups):
        value = value + band_in[d - 1]
    y_in[y] = value

    copies = []
    for d in range(1, YS):
        copies.append(remote(y_in.at[y], y_in.at[y], y_send.at[d - 1], y_recv.at[d - 1], y_peer(d)))
        copies[-1].start()
    finish(copies)
    value = y_in[0]
    for k in range(1, YS):
        value = value + y_in[k]
    z_in[z] = value

    copies = []
    for d in range(1, ZS):
        copies.append(remote(z_in.at[z], z_in.at[z], z_send.at[d - 1], z_recv.at[d - 1], z_peer(d)))
        copies[-1].start()
    finish(copies)
    value = z_in[0]
    for k in range(1, ZS):
        value = value + z_in[k]
    whole[core, band] = value

    copies = []
    for d in range(1, groups):
        piece = whole.at[core, band]
        copies.append(remote(piece, piece, g_send.at[d - 1], g_recv.at[d - 1], band_peer(d)))
        copies[-1].start()
    finish(copies)
    copy = remote(whole.at[core], whole.at[core], c_send.at[1], c_recv.at[1], twin)
    copy.start()
    copy.wait()

    mat[...] = whole[...].reshape(count, wide) / total_nodes
    factor_inverse(mat)
    row = lax.broadcasted_iota(jnp.int32, (count, wide), 0)
    column = lax.broadcasted_iota(jnp.int32, (count, wide), 1)
    high, low = split(jnp.where(column <= row, mat[...], 0.0))
    filtered = rows_all[...]
    result = nn(high, filtered) + nn(low, filtered)
    ortho[...] = result.astype(BF).reshape(ortho.shape)

    copies = []
    for d in range(1, groups):
        there = band_peer(d)
        copies.append(remote(ortho.at[there["band"]], back.at[band], b_send.at[d - 1], b_recv.at[d - 1], there))
        copies[-1].start()
    back[band] = ortho[band]
    finish(copies)
    nodes = out_ref.shape[1]
    for k in range(groups):
        size = min(width, nodes - k * width)
        if size > 0:
            out_ref[:, k * width:k * width + size] = back[k, :, 0:size].astype(F32)


def per_device(psi, ham, conn, face_rows):
    bands, nodes = psi.shape
    elems = conn.shape[0]
    faces = face_rows.shape[0]
    groups = lax.axis_size("band")
    own_blocks = pl.cdiv(nodes, LO)
    ghost_blocks = pl.cdiv(faces, LO)
    face_pad = pl.cdiv(faces, 128) * 128
    width = pl.cdiv(pl.cdiv(nodes, 128), groups) * 128
    own = own_blocks * bands
    entries = elems * NODE_EL
    vmem = pl.BlockSpec(memory_space=pltpu.VMEM)
    dma = pltpu.SemaphoreType.DMA

    filtered = pl.pallas_call(
        filter_kernel,
        out_shape=jax.ShapeDtypeStruct((groups, bands, width), BF),
        in_specs=[vmem] * 4,
        out_specs=vmem,
        scratch_shapes=[
            pltpu.VMEM((LO, entries), BF),
            pltpu.VMEM((LO, face_pad), BF),
            pltpu.VMEM((bands, entries), jnp.int32),
            pltpu.VMEM((bands, face_pad), jnp.int32),
            pltpu.VMEM((own, LO), F32),
            pltpu.VMEM((own, LO), F32),
            pltpu.VMEM((own + ghost_blocks * bands, LO), F32),
            pltpu.VMEM((own, LO), BF),
            pltpu.VMEM((ghost_blocks * bands, LO), BF),
            pltpu.VMEM((bands, entries), BF),
            pltpu.VMEM((bands, entries), F32),
            pltpu.VMEM((bands, face_pad), BF),
            pltpu.VMEM((bands, face_pad), F32),
            pltpu.VMEM((bands, face_pad), F32),
            pltpu.VMEM((bands, face_pad), F32),
            pltpu.VMEM((bands, face_pad), BF),
            pltpu.VMEM((bands, face_pad), F32),
            pltpu.VMEM((bands, face_pad), F32),
            pltpu.VMEM((bands, face_pad), F32),
            dma((4,)),
            dma((4,)),
        ],
        compiler_params=pltpu.CompilerParams(
            collective_id=0, has_side_effects=True, vmem_limit_bytes=VMEM_LIMIT
        ),
        name="filter",
    )(psi, ham, conn, face_rows.reshape(1, faces))

    count = groups * bands
    wide = pl.cdiv(count, 128) * 128
    unit = count // CORES // groups
    return pl.pallas_call(
        functools.partial(tail_kernel, float(nodes * lax.axis_size("space"))),
        out_shape=jax.ShapeDtypeStruct((bands, nodes), F32),
        in_specs=[vmem],
        out_specs=vmem,
        scratch_shapes=[
            pltpu.VMEM((wide, width), BF),
            pltpu.VMEM((count, wide), F32),
            pltpu.VMEM((count // CORES, wide), F32),
            pltpu.VMEM((groups, unit, wide), F32),
            pltpu.VMEM((groups - 1, unit, wide), F32),
            pltpu.VMEM((YS, unit, wide), F32),
            pltpu.VMEM((ZS, unit, wide), F32),
            pltpu.VMEM((CORES, groups, unit, wide), F32),
            pltpu.VMEM((count, wide), F32),
            pltpu.VMEM((groups, bands, width), BF),
            pltpu.VMEM((groups, bands, width), BF),
            dma((groups - 1,)), dma((groups - 1,)),
            dma((2,)), dma((2,)),
            dma((groups - 1,)), dma((groups - 1,)),
            dma((YS - 1,)), dma((YS - 1,)),
            dma((ZS - 1,)), dma((ZS - 1,)),
            dma((groups - 1,)), dma((groups - 1,)),
            dma((groups - 1,)), dma((groups - 1,)),
        ],
        compiler_params=pltpu.CompilerParams(
            collective_id=1, has_side_effects=True, vmem_limit_bytes=VMEM_LIMIT
        ),
        name="tail",
    )(filtered)


def solution(mesh):
    placed = (P("band", "space"), P("space", None, None), P("space", None), P("space"))
    return jax.shard_map(
        per_device, mesh=mesh, in_specs=placed, out_specs=P("band", "space"), check_vma=False
    )
```

time: 767 us -> 111 us (0.14)
  waiting for transfers between devices: 475 us -> 0 us
  other arithmetic: 148 us -> 0 us
  Pallas kernels: 0 us -> 106 us
  local copies, waits for them, and re-layouts: 66.3 us -> 2.94 us
  starting transfers between devices: 35.8 us -> 0 us
  between operations: 15.1 us -> 0.02 us
  blocking collectives: 12.7 us -> 0 us
  matrix products: 10.5 us -> 0 us
    psum x1 -> x0, waiting for transfers between devices: 443 us -> none  [per_device(): correlation = lax.psum(partial_value, ('space', 'band'))]
    pallas_call x0 -> x2, Pallas kernels: none -> 106 us  [the longest x1 55.6 us: per_device(): pl.pallas_call(functools.partial(tail_kernel, float(nodes * lax.axis_size...]
    scatter-add x4 -> x0, other arithmetic: 86.2 us -> none  [the longest x2 68.1 us: apply_operator(): summed.at[:, flat_conn]]
    another operation x14 -> x0, other arithmetic: 48.6 us -> none  [the longest x7 28.8 us: per_device(): factor = jnp.linalg.cholesky(correlation)]
    gather x5 -> x0, local copies, waits for them, and re-layouts: 48.1 us -> none  [the longest x2 44.1 us: apply_operator(): jnp.take(extended, flat_conn, axis=1)]
    ppermute x4 -> x0, waiting for transfers between devices: 25.7 us -> none  [from_behind(): return lax.ppermute(block, axis, route)]
    ppermute x4 -> x0, starting transfers between devices: 22.9 us -> none  [from_behind(): return lax.ppermute(block, axis, route)]
    all_to_all x1 -> x0, starting transfers between devices: 13 us -> none  [per_device(): lax.all_to_all(following, 'band', split_axis=1, concat_axis=0, tiled=True)]
  transfers between devices with their start and end apart: 6 -> 0, of which waited for: 6 -> 0; matrix products, arithmetic and copies ran while one was open for 1% -> 0% of each run, Pallas kernels for 0% -> 0%
where the time goes in v1:
time: 111 us; the launch traced here: 109 us
  Pallas kernels  106 us (95%)
  local copies, waits for them, and re-layouts  2.94 us (3%)
    pallas_call x1, Pallas kernels, per_device(): pl.pallas_call(functools.partial(tail_kernel, float(nodes * lax.axis_size...  55.6 us
    pallas_call x1, Pallas kernels, per_device(): pl.pallas_call(filter_kernel, out_shape=jax.ShapeDtypeStruct((groups, ban...  50.7 us

profile of v1, /device:TPU:6, one launch (start us, length us, event | category | flops | bytes accessed | tf_op | source)
XLA Modules:
  0.0 109.3 jit_solution(11205339314021760201)
XLA Ops:
  0.0 1.3 %reshape.3.face_ref = s32[1,588]{1,0:T(1,128)} reshape(s32[588]{0:T(1024)} %param.7) | data formatting | bytes 4704 | tf_op jit(solution)/shard_map/reshape | solution.py:433
  1.3 50.7 %filter.1.in_ref = bf16[12,16,384]{2,1,0:T(8,128)(2,1)} custom-call(f32[16,4116]{1,0:T(8,128)} %psi_ref.1, bf16[12,512,512]{2,1,0:T(8,128)(2,1)} %ham_ref.1, s32[12,512]{1,0:T(8,128)} %conn_ref.1, s32[1,588]{1,0:T(1,128)} %reshape.3.face_ref), custom_call_target="tpu_custom_call" | custom-call | tf_op jit(solution)/shard_map/filter/pallas_call | solution.py:401
  52.0 55.6 %tail.1 = f32[16,4116]{1,0:T(8,128)} custom-call(bf16[12,16,384]{2,1,0:T(8,128)(2,1)} %filter.1.in_ref), custom_call_target="tpu_custom_call" | custom-call | tf_op jit(solution)/shard_map/tail/pallas_call | solution.py:438
  107.6 1.7 %copy.6 = f32[16,4116]{1,0:T(8,128)} copy(f32[16,4116]{1,0:T(8,128)} %tail.1) | data formatting | bytes 526848

commit v2 on v0

v2 whole, which is shorter than its diff:
```python
import functools

import jax
import jax.numpy as jnp
from jax import lax
from jax.experimental import pallas as pl
from jax.experimental.pallas import tpu as pltpu
from jax.sharding import PartitionSpec as P

NODE_EL = 512
OWN_EL = 448
CENTER = 6.25
HALF_WIDTH = 7.5
LO = 256
TAIL = 128
MESH = pl.DeviceIdType.MESH
BF = jnp.bfloat16
F32 = jnp.float32
VMEM_LIMIT = 60 * 1024 * 1024

CORES, YS, ZS = 2, 8, 4
HAM_PARTS = 4
NT = (((1,), (1,)), ((), ()))
TN = (((0,), (0,)), ((), ()))


def nn(a, b):
    return jnp.dot(a, b, preferred_element_type=F32)


def nt(a, b):
    return lax.dot_general(a, b, NT, preferred_element_type=F32)


def remote(src, dst, send, recv, where):
    return pltpu.make_async_remote_copy(
        src_ref=src, dst_ref=dst, send_sem=send, recv_sem=recv, device_id=where, device_id_type=MESH
    )


def split(value):
    high = value.astype(BF)
    return high, (value - high.astype(F32)).astype(BF)


def split3(value):
    high = value.astype(BF)
    rest = value - high.astype(F32)
    middle = rest.astype(BF)
    return high, middle, (rest - middle.astype(F32)).astype(BF)


def lanes(start, size):
    return pl.ds(pl.multiple_of(start, 128), size)


def pick(table, which, first, count, total):
    bands = total.shape[0]
    for h in range(count):
        total = jnp.where(which == first + h, table[h * bands:(h + 1) * bands, :], total)
    return total


def place(parts, which, first, count, columns):
    zero = jnp.zeros_like(parts[0])
    keep = [which == first + h for h in range(count)]
    rows = [jnp.where(k, part, zero) for part in parts for k in keep]
    result = nt(jnp.concatenate(rows, axis=0), columns)
    size = result.shape[0] // len(parts)
    return sum(result[n * size:(n + 1) * size] for n in range(1, len(parts))) + result[0:size]


def indicator(low, depth):
    shape = depth.shape
    return jnp.where(depth == jnp.broadcast_to(low, shape), jnp.ones(shape, BF), jnp.zeros(shape, BF))


def as_bf(value, rows):
    return jnp.broadcast_to(value.astype(F32), (rows, value.shape[1])).astype(BF)


def factor_inverse(mat, panel=32):
    size, wide = mat.shape
    step = 8
    lane = lax.broadcasted_iota(jnp.int32, (step, 128), 1)
    sub = lax.broadcasted_iota(jnp.int32, (step, 128), 0)
    tiles = range(wide // 128)

    def spread_lane(value, j):
        return jnp.broadcast_to(value[:, j:j + 1], (step, 128))

    def spread_row(value, i):
        return jnp.broadcast_to(value[i:i + 1, :], (step, 128))

    for top in range(0, size, panel):
        groups = min(panel, size - top) // step
        block = [
            [mat[top + step * g:top + step * (g + 1), t * 128:(t + 1) * 128] for t in tiles] for g in range(groups)
        ]
        for s in range(groups):
            start = top + step * s
            tile, at = start // 128, start % 128
            columns = [spread_lane(block[s][tile], at + j) for j in range(step)]
            d = {(i, j): spread_row(columns[j], i) for j in range(step) for i in range(j, step)}
            below = [[spread_lane(block[g][tile], at + j) for j in range(step)] for g in range(s + 1, groups)]
            inside = (lane >= at) & (lane < at + step)
            base = [[spread_row(block[s][t], i) for i in range(step)] for t in tiles]
            for i in range(step):
                base[tile][i] = jnp.where(inside, jnp.where(lane == at + i, 1.0, 0.0), base[tile][i])
            rows = [[] for _ in tiles]
            for k in range(step):
                scale = lax.rsqrt(d[k, k])
                factor = {i: d[i, k] * scale for i in range(k + 1, step)}
                for i in range(k + 1, step):
                    for m in range(k + 1, i + 1):
                        d[i, m] = d[i, m] - factor[i] * factor[m]
                for t in tiles:
                    rows[t].append(base[t][k] * scale)
                    for i in range(k + 1, step):
                        base[t][i] = base[t][i] - factor[i] * rows[t][k]
                for part in below:
                    part[k] = part[k] * scale
                    for i in range(k + 1, step):
                        part[i] = part[i] - part[k] * factor[i]
            for t in tiles:
                fresh = rows[t][0]
                for i in range(1, step):
                    fresh = jnp.where(sub == i, rows[t][i], fresh)
                block[s][t] = fresh
            for n, g in enumerate(range(s + 1, groups)):
                for t in tiles:
                    value = block[g][t]
                    if t == tile:
                        value = jnp.where(inside, 0.0, value)
                    for k in range(step):
                        value = value - below[n][k] * rows[t][k]
                    block[g][t] = value
        for g in range(groups):
            for t in tiles:
                mat[top + step * g:top + step * (g + 1), t * 128:(t + 1) * 128] = block[g][t]
        end = top + step * groups
        if end < size:
            first = end // 128 * 128
            fresh = mat[top:end, :]
            row = top + lax.broadcasted_iota(jnp.int32, fresh.shape, 0)
            column = lax.broadcasted_iota(jnp.int32, fresh.shape, 1)
            a, b, c = split3(fresh[:, first:])
            d, e, f = split3(jnp.where((column > row) & (column < end), 0.0, fresh))
            update = lax.dot_general(
                jnp.concatenate([a, a, b, b, a, c], axis=0),
                jnp.concatenate([d, e, d, e, f, d], axis=0),
                TN,
                preferred_element_type=F32,
            )
            rest = mat[end:size, :]
            column = lax.broadcasted_iota(jnp.int32, rest.shape, 1)
            rest = jnp.where((column >= top) & (column < end), 0.0, rest)
            mat[end:size, :] = rest - update[end - first:size - first, :]


def step_kernel(
    total_nodes, psi_ref, ham_hbm, conn_ref, face_ref, out_ref,
    ham, onehot, onehot_ghost, onehot_face, hi_ref, hi_ghost, hi_face, base, field, xb, xg,
    gathered, high_ref, low_ref,
    send1, send2, send3, send4, got1, got2, got3, got4,
    pieces, rows_all, gram, half_in, half, band_in, y_in, z_in, whole, mat, ortho,
    ham_sem, own_sem, f_send, f_recv, a_send, a_recv, c_send, c_recv, r_send, r_recv, y_send, y_recv, z_send, z_recv,
    g_send, g_recv, t_send, t_recv, b_send, b_recv,
):
    bands, nodes = psi_ref.shape
    elems = conn_ref.shape[0]
    faces = face_ref.shape[0]
    own_blocks = pl.cdiv(nodes, LO)
    ghost_blocks = pl.cdiv(faces, LO)
    face_pad = got1.shape[1]
    shift = own_blocks * LO - nodes
    domains = lax.axis_size("space")
    space = lax.axis_index("space")
    band = lax.axis_index("band")
    groups, _, width = pieces.shape
    count = groups * bands
    wide = mat.shape[1]
    core = lax.rem(space, CORES)
    y = lax.rem(space // CORES, YS)
    z = space // (CORES * YS)
    below = {"space": lax.rem(space + domains - 1, domains)}
    above = {"space": lax.rem(space + 1, domains)}
    twin = {"space": space + 1 - 2 * core}

    def band_peer(d):
        return {"band": lax.rem(band + d, groups)}

    def y_peer(d):
        return {"space": (z * YS + lax.rem(y + d, YS)) * CORES + core}

    def z_peer(d):
        return {"space": (lax.rem(z + d, ZS) * YS + y) * CORES + core}

    peers = [below, above, twin]
    peers += [band_peer(d) for d in range(1, groups)]
    peers += [y_peer(d) for d in range(1, YS)]
    peers += [z_peer(d) for d in range(1, ZS)]
    barrier = pltpu.get_barrier_semaphore()
    for there in peers:
        pl.semaphore_signal(barrier, inc=1, device_id=there, device_id_type=MESH)

    per = elems // HAM_PARTS
    ham_copies = []
    for k in range(HAM_PARTS):
        part = slice(k * per, (k + 1) * per)
        ham_copies.append(pltpu.make_async_copy(ham_hbm.at[part], ham.at[part], ham_sem.at[k]))
        ham_copies[-1].start()

    for h in range(own_blocks):
        rows = slice(h * bands, (h + 1) * bands)
        if (h + 1) * LO <= nodes:
            value = psi_ref[:, h * LO:(h + 1) * LO]
            base[rows, :] = value
            xb[rows, :] = value.astype(BF)
        else:
            base[rows, :] = jnp.zeros((bands, LO), F32)
            base[rows, 0:nodes - h * LO] = psi_ref[:, h * LO:nodes]
            xb[rows, :] = base[rows, :].astype(BF)

    depth = lax.broadcasted_iota(jnp.int32, (LO, NODE_EL), 0).astype(F32).astype(BF)
    for k in range(face_pad // 128):
        size = min(128, faces - k * 128)
        named = jnp.full((1, 128), -1, jnp.int32)
        spot = lax.broadcasted_iota(jnp.int32, (1, 128), 1)
        if size == 128:
            named = face_ref[k * 128:(k + 1) * 128].reshape(1, 128)
        else:
            tail = face_ref[faces - 128:faces].reshape(1, 128)
            named = jnp.where(spot < size, pltpu.roll(tail, size, 1), -1)
        cols = slice(k * 128, (k + 1) * 128)
        onehot_face[:, cols] = indicator(as_bf(named & (LO - 1), 1), depth[:, 0:128])
        hi_face[:, cols] = as_bf(named >> 8, bands)

    def take_face(blocks):
        table = nn(blocks, onehot_face[...]).astype(BF)
        return pick(table, hi_face[...], 0, own_blocks, jnp.zeros((bands, face_pad), BF))

    send1[...] = take_face(xb[...])
    pl.semaphore_wait(barrier, len(peers))
    copy1 = remote(send1, got1, f_send.at[0], f_recv.at[0], below)
    copy1.start()

    spot = lax.broadcasted_iota(jnp.int32, (1, NODE_EL), 1)

    def prepare(e, carry):
        named = conn_ref[pl.ds(e, 1), :]
        named = jnp.where(spot >= OWN_EL, named + shift, named)
        marks = indicator(as_bf(named & (LO - 1), 1), depth)
        which = as_bf(named >> 8, bands)
        cols = lanes(e * NODE_EL, NODE_EL)
        onehot[:, cols] = marks
        hi_ref[:, cols] = which
        cols = lanes(e * TAIL, TAIL)
        onehot_ghost[:, cols] = marks[:, NODE_EL - TAIL:]
        hi_ghost[:, cols] = which[:, NODE_EL - TAIL:]
        return carry

    lax.fori_loop(0, elems, prepare, 0, unroll=2)
    xg[...] = jnp.zeros(xg.shape, BF)
    rows_all[count:, :] = jnp.zeros((rows_all.shape[0] - count, width), BF)

    def gather_own():
        def body(e, carry):
            cols = lanes(e * NODE_EL, NODE_EL)
            table = nn(xb[...], onehot[:, cols]).astype(BF)
            gathered[:, cols] = pick(table, hi_ref[:, cols], 0, own_blocks, jnp.zeros((bands, NODE_EL), BF))
            return carry

        lax.fori_loop(0, elems, body, 0, unroll=4)

    def gather_ghost(values):
        for h in range(ghost_blocks):
            size = min(LO, face_pad - h * LO)
            xg[h * bands:(h + 1) * bands, 0:size] = values[:, h * LO:h * LO + size].astype(BF)
        table = nn(xg[...], onehot_ghost[...]).astype(BF)
        found = pick(table, hi_ghost[...], own_blocks, ghost_blocks, jnp.zeros((bands, elems * TAIL), BF))
        for e in range(elems):
            cols = slice((e + 1) * NODE_EL - TAIL, (e + 1) * NODE_EL)
            gathered[:, cols] = gathered[:, cols] + found[:, e * TAIL:(e + 1) * TAIL]

    def multiply():
        def body(e, carry):
            cols = lanes(e * NODE_EL, NODE_EL)
            high_ref[:, cols], low_ref[:, cols] = split(nn(gathered[:, cols], ham[e]))
            return carry

        lax.fori_loop(0, elems, body, 0, unroll=4)

    def upper():
        cols = [slice((e + 1) * NODE_EL - TAIL, (e + 1) * NODE_EL) for e in range(elems)]
        high = jnp.concatenate([high_ref[:, c] for c in cols], axis=1)
        low = jnp.concatenate([low_ref[:, c] for c in cols], axis=1)
        total = place([high, low], hi_ghost[...], own_blocks, ghost_blocks, onehot_ghost[...])
        parts = [
            total[h * bands:(h + 1) * bands, 0:min(LO, face_pad - h * LO)] for h in range(ghost_blocks)
        ]
        return jnp.concatenate(parts, axis=1)

    def scatter_own():
        half_cols = elems * NODE_EL // 2
        total = None
        for k in range(2):
            cols = slice(k * half_cols, (k + 1) * half_cols)
            value = place([high_ref[:, cols], low_ref[:, cols]], hi_ref[:, cols], 0, own_blocks, onehot[:, cols])
            total = value if total is None else total + value
        return total

    def put_face(received):
        return place(list(split(received)), hi_face[...], 0, own_blocks, onehot_face[...])

    gather_own()
    copy1.wait()
    gather_ghost(got1[...])
    for c in ham_copies:
        c.wait()
    multiply()
    send2[...] = upper()
    copy2 = remote(send2, got2, f_send.at[1], f_recv.at[1], above)
    copy2.start()
    partial_value = (scatter_own() - CENTER * base[...]) / HALF_WIDTH
    field[...] = partial_value
    high, low = split(partial_value)
    send3[...] = take_face(high).astype(F32) + take_face(low).astype(F32)
    copy3 = remote(send3, got3, f_send.at[2], f_recv.at[2], below)
    copy3.start()
    copy2.wait()
    field[...] += put_face(got2[...] / HALF_WIDTH)
    xb[...] = field[...].astype(BF)
    gather_own()
    copy3.wait()
    gather_ghost(got3[...] + send2[...] / HALF_WIDTH)
    multiply()
    send4[...] = upper()
    copy4 = remote(send4, got4, f_send.at[3], f_recv.at[3], above)
    copy4.start()
    partial_value = scatter_own() - CENTER * field[...]
    copy4.wait()
    field[...] = 2.0 * ((partial_value + put_face(got4[...])) / HALF_WIDTH) - base[...]

    blocks = width // 128
    for piece in range(groups * blocks):
        dst = slice((piece % blocks) * 128, (piece % blocks + 1) * 128)
        if piece // 2 < own_blocks:
            rows = slice(piece // 2 * bands, (piece // 2 + 1) * bands)
            src = slice((piece % 2) * 128, (piece % 2 + 1) * 128)
            pieces[piece // blocks, :, dst] = field[rows, src].astype(BF)
        else:
            pieces[piece // blocks, :, dst] = jnp.zeros((bands, 128), BF)

    def finish(copies):
        for c in copies:
            c.wait()

    mine = pl.ds(pl.multiple_of(band * bands, bands), bands)
    copies = []
    for d in range(1, groups):
        there = band_peer(d)
        copies.append(remote(pieces.at[there["band"]], rows_all.at[mine], a_send.at[d - 1], a_recv.at[d - 1], there))
        copies[-1].start()
    rows_all[mine, :] = pieces[band]
    finish(copies)

    part = count // CORES
    theirs = pl.ds(pl.multiple_of((1 - core) * part, 16), part)
    ours = pl.ds(pl.multiple_of(core * part, 16), part)
    gram[0] = nt(rows_all[theirs, :], rows_all[...])
    copy = remote(gram.at[0], half_in, c_send.at[0], c_recv.at[0], twin)
    copy.start()
    gram[1] = nt(rows_all[ours, :], rows_all[...])
    copy.wait()
    half[...] = (gram[1] + half_in[...]).reshape(half.shape)

    copies = []
    for d in range(1, groups):
        there = band_peer(d)
        copies.append(remote(half.at[there["band"]], band_in.at[d - 1], r_send.at[d - 1], r_recv.at[d - 1], there))
        copies[-1].start()
    finish(copies)
    value = half[band]
    for d in range(1, groups):
        value = value + band_in[d - 1]
    y_in[y] = value

    copies = []
    for d in range(1, YS):
        copies.append(remote(y_in.at[y], y_in.at[y], y_send.at[d - 1], y_recv.at[d - 1], y_peer(d)))
        copies[-1].start()
    finish(copies)
    value = y_in[0]
    for k in range(1, YS):
        value = value + y_in[k]
    z_in[z] = value

    copies = []
    for d in range(1, ZS):
        copies.append(remote(z_in.at[z], z_in.at[z], z_send.at[d - 1], z_recv.at[d - 1], z_peer(d)))
        copies[-1].start()
    finish(copies)
    value = z_in[0]
    for k in range(1, ZS):
        value = value + z_in[k]
    whole[core, band] = value

    copies = {}
    piece = whole.at[core, band]
    for d in range(1, groups):
        copies[d] = remote(piece, piece, g_send.at[d - 1], g_recv.at[d - 1], band_peer(d))
        copies[d].start()
    forwarded = [remote(piece, piece, t_send.at[0], t_recv.at[0], twin)]
    forwarded[0].start()
    for d in sorted(copies, key=lambda d: (min(d, groups - d) not in (1, 3), d)):
        copies[d].wait_recv()
        piece = whole.at[core, lax.rem(band + groups - d, groups)]
        forwarded.append(remote(piece, piece, t_send.at[d], t_recv.at[d], twin))
        forwarded[-1].start()
    for d in copies:
        copies[d].wait_send()
    finish(forwarded)

    mat[...] = whole[...].reshape(count, wide) / total_nodes
    factor_inverse(mat)
    row = lax.broadcasted_iota(jnp.int32, (count, wide), 0)
    column = lax.broadcasted_iota(jnp.int32, (count, wide), 1)
    high, low = split(jnp.where(column <= row, mat[...], 0.0))
    filtered = rows_all[...]
    result = nn(high, filtered) + nn(low, filtered)
    ortho[...] = result.astype(BF).reshape(ortho.shape)

    copies = []
    landing = out_ref.at[:, lanes(band * width, width)]
    for d in range(1, groups):
        there = band_peer(d)
        copies.append(remote(ortho.at[there["band"]], landing, b_send.at[d - 1], b_recv.at[d - 1], there))
        copies[-1].start()
    copy = pltpu.make_async_copy(ortho.at[band], landing, own_sem)
    copy.start()
    copy.wait()
    finish(copies)


def per_device(psi, ham, conn, face_rows):
    bands, nodes = psi.shape
    elems = conn.shape[0]
    faces = face_rows.shape[0]
    groups = lax.axis_size("band")
    own_blocks = pl.cdiv(nodes, LO)
    ghost_blocks = pl.cdiv(faces, LO)
    face_pad = pl.cdiv(faces, 128) * 128
    width = pl.cdiv(pl.cdiv(nodes, 128), groups) * 128
    own = own_blocks * bands
    entries = elems * NODE_EL
    count = groups * bands
    wide = pl.cdiv(count, 128) * 128
    unit = count // CORES // groups
    vmem = pl.BlockSpec(memory_space=pltpu.VMEM)
    anywhere = pl.BlockSpec(memory_space=pl.ANY)
    dma = pltpu.SemaphoreType.DMA

    result = pl.pallas_call(
        functools.partial(step_kernel, float(nodes * lax.axis_size("space"))),
        out_shape=jax.ShapeDtypeStruct((bands, groups * width), BF),
        in_specs=[vmem, anywhere, vmem, vmem],
        out_specs=anywhere,
        scratch_shapes=[
            pltpu.VMEM(ham.shape, BF),
            pltpu.VMEM((LO, entries), BF),
            pltpu.VMEM((LO, elems * TAIL), BF),
            pltpu.VMEM((LO, face_pad), BF),
            pltpu.VMEM((bands, entries), BF),
            pltpu.VMEM((bands, elems * TAIL), BF),
            pltpu.VMEM((bands, face_pad), BF),
            pltpu.VMEM((own, LO), F32),
            pltpu.VMEM((own, LO), F32),
            pltpu.VMEM((own, LO), BF),
            pltpu.VMEM((ghost_blocks * bands, LO), BF),
            pltpu.VMEM((bands, entries), BF),
            pltpu.VMEM((bands, entries), BF),
            pltpu.VMEM((bands, entries), BF),
            pltpu.VMEM((bands, face_pad), BF),
            pltpu.VMEM((bands, face_pad), F32),
            pltpu.VMEM((bands, face_pad), F32),
            pltpu.VMEM((bands, face_pad), F32),
            pltpu.VMEM((bands, face_pad), BF),
            pltpu.VMEM((bands, face_pad), F32),
            pltpu.VMEM((bands, face_pad), F32),
            pltpu.VMEM((bands, face_pad), F32),
            pltpu.VMEM((groups, bands, width), BF),
            pltpu.VMEM((wide, width), BF),
            pltpu.VMEM((CORES, count // CORES, wide), F32),
            pltpu.VMEM((count // CORES, wide), F32),
            pltpu.VMEM((groups, unit, wide), F32),
            pltpu.VMEM((groups - 1, unit, wide), F32),
            pltpu.VMEM((YS, unit, wide), F32),
            pltpu.VMEM((ZS, unit, wide), F32),
            pltpu.VMEM((CORES, groups, unit, wide), F32),
            pltpu.VMEM((count, wide), F32),
            pltpu.VMEM((groups, bands, width), BF),
            dma((HAM_PARTS,)), dma,
            dma((4,)), dma((4,)),
            dma((groups - 1,)), dma((groups - 1,)),
            dma((1,)), dma((1,)),
            dma((groups - 1,)), dma((groups - 1,)),
            dma((YS - 1,)), dma((YS - 1,)),
            dma((ZS - 1,)), dma((ZS - 1,)),
            dma((groups - 1,)), dma((groups - 1,)),
            dma((groups,)), dma((groups,)),
            dma((groups - 1,)), dma((groups - 1,)),
        ],
        compiler_params=pltpu.CompilerParams(
            collective_id=0, has_side_effects=True, vmem_limit_bytes=VMEM_LIMIT
        ),
        name="step",
    )(psi, ham, conn, face_rows)
    return result[:, 0:nodes].astype(F32)


def solution(mesh):
    placed = (P("band", "space"), P("space", None, None), P("space", None), P("space"))
    return jax.shard_map(
        per_device, mesh=mesh, in_specs=placed, out_specs=P("band", "space"), check_vma=False
    )
```

time: 767 us -> 78.4 us (0.10)
  waiting for transfers between devices: 475 us -> 0 us
  other arithmetic: 148 us -> 1.63 us
  Pallas kernels: 0 us -> 75.4 us
  local copies, waits for them, and re-layouts: 66.3 us -> 0 us
  starting transfers between devices: 35.8 us -> 0 us
  between operations: 15.1 us -> 0.01 us
  blocking collectives: 12.7 us -> 0 us
  matrix products: 10.5 us -> 0 us
    psum x1 -> x0, waiting for transfers between devices: 443 us -> none  [per_device(): correlation = lax.psum(partial_value, ('space', 'band'))]
    scatter-add x4 -> x0, other arithmetic: 86.2 us -> none  [the longest x2 68.1 us: apply_operator(): summed.at[:, flat_conn]]
    pallas_call x0 -> x1, Pallas kernels: none -> 75.4 us  [per_device(): pl.pallas_call(functools.partial(step_kernel, float(nodes * lax.axis_size...]
    another operation x14 -> x0, other arithmetic: 48.6 us -> none  [the longest x7 28.8 us: per_device(): factor = jnp.linalg.cholesky(correlation)]
    gather x5 -> x0, local copies, waits for them, and re-layouts: 48.1 us -> none  [the longest x2 44.1 us: apply_operator(): jnp.take(extended, flat_conn, axis=1)]
    ppermute x4 -> x0, waiting for transfers between devices: 25.7 us -> none  [from_behind(): return lax.ppermute(block, axis, route)]
    ppermute x4 -> x0, starting transfers between devices: 22.9 us -> none  [from_behind(): return lax.ppermute(block, axis, route)]
    all_to_all x1 -> x0, starting transfers between devices: 13 us -> none  [per_device(): lax.all_to_all(following, 'band', split_axis=1, concat_axis=0, tiled=True)]
  transfers between devices with their start and end apart: 6 -> 0, of which waited for: 6 -> 0; matrix products, arithmetic and copies ran while one was open for 1% -> 0% of each run, Pallas kernels for 0% -> 0%
where the time goes in v2:
time: 78.4 us; the launch traced here: 77 us
  Pallas kernels  75.4 us (96%)
  other arithmetic  1.63 us (2%)
    pallas_call x1, Pallas kernels, per_device(): pl.pallas_call(functools.partial(step_kernel, float(nodes * lax.axis_size...  75.4 us
    convert_element_type x1, other arithmetic, per_device(): return result[:, 0:nodes].astype(F32)  1.63 us

profile of v2, /device:TPU:6, one launch (start us, length us, event | category | flops | bytes accessed | tf_op | source)
XLA Modules:
  0.0 77.0 jit_solution(7075689779703308129)
XLA Ops:
  0.0 75.4 %step.1 = bf16[16,4608]{1,0:T(8,128)(2,1)} custom-call(f32[16,4116]{1,0:T(8,128)} %psi_ref.1, bf16[12,512,512]{2,1,0:T(8,128)(2,1)} %ham_hbm.1, s32[12,512]{1,0:T(8,128)} %conn_ref.1, s32[588]{0:T(1024)} %face_ref.1), custom_call_target="tpu_custom_call" | custom-call | tf_op jit(solution)/shard_map/step/pallas_call | solution.py:464
  75.4 1.6 %slice_convert_fusion = f32[16,4116]{1,0:T(8,128)} fusion(bf16[16,4608]{1,0:T(8,128)(2,1)} %step.1), kind=kLoop, calls=%fused_computation | loop fusion | flops 65856 | bytes 395136 | tf_op jit(solution)/shard_map/convert_element_type | solution.py:519

commit v3 on v2

--- a/solution.py
+++ b/solution.py
@@ -79,7 +79,7 @@
     return jnp.broadcast_to(value.astype(F32), (rows, value.shape[1])).astype(BF)
 
 
-def factor_inverse(mat, panel=32):
+def factor_inverse(mat, panel, beside, after):
     size, wide = mat.shape
     step = 8
     lane = lax.broadcasted_iota(jnp.int32, (step, 128), 1)
@@ -93,6 +93,8 @@
         return jnp.broadcast_to(value[i:i + 1, :], (step, 128))
 
     for top in range(0, size, panel):
+        if top > 0:
+            beside(top - panel, top)
         groups = min(panel, size - top) // step
         block = [
             [mat[top + step * g:top + step * (g + 1), t * 128:(t + 1) * 128] for t in tiles] for g in range(groups)
@@ -156,6 +158,39 @@
             column = lax.broadcasted_iota(jnp.int32, rest.shape, 1)
             rest = jnp.where((column >= top) & (column < end), 0.0, rest)
             mat[end:size, :] = rest - update[end - first:size - first, :]
+        if top > 0:
+            after(top - panel, top)
+
+
+def fold(matrix):
+    half = matrix.shape[0] // 2
+    upper, lower = matrix[0:half, :], matrix[half:, :]
+    row = lax.broadcasted_iota(jnp.int32, lower.shape, 0)
+    lane = lax.broadcasted_iota(jnp.int32, lower.shape, 1)
+    diagonal = jnp.sum(jnp.where(lane == row + half, lower, 0.0), axis=1, keepdims=True)
+    mixed = jnp.where((lane >= half) & (lane - half <= row), pltpu.roll(upper, half, 1), lower)
+    return jnp.where(lane < 2 * half, mixed, diagonal)
+
+
+def unfold(folded):
+    half, wide = folded.shape
+    row = lax.broadcasted_iota(jnp.int32, folded.shape, 0)
+    lane = lax.broadcasted_iota(jnp.int32, folded.shape, 1)
+    diagonal = jnp.broadcast_to(folded[:, 2 * half:2 * half + 1], folded.shape)
+    mixed = pltpu.roll(folded, wide - half, 1)
+    zeros = jnp.zeros((128 - half, 128), F32)
+
+    def flip(value):
+        square = jnp.concatenate([value[:, 0:128], zeros], axis=0).T[0:half, :]
+        return jnp.concatenate([square, jnp.zeros((half, wide - 128), F32)], axis=1)
+
+    other = flip(jnp.where(lane < half, mixed, 0.0))
+    corner = flip(jnp.where(lane < half, folded, 0.0))
+    first = jnp.where(lane < half, jnp.where(lane <= row, mixed, other), pltpu.roll(corner, half, 1))
+    last = jnp.where(lane == row, diagonal, jnp.where(lane > row, mixed, other))
+    last = jnp.where(lane < half, folded, pltpu.roll(last, half, 1))
+    inside = lane < 2 * half
+    return jnp.where(inside, first, 0.0), jnp.where(inside, last, 0.0)
 
 
 def step_kernel(
@@ -163,9 +198,9 @@
     ham, onehot, onehot_ghost, onehot_face, hi_ref, hi_ghost, hi_face, base, field, xb, xg,
     gathered, high_ref, low_ref,
     send1, send2, send3, send4, got1, got2, got3, got4,
-    pieces, rows_all, gram, half_in, half, band_in, y_in, z_in, whole, mat, ortho,
-    ham_sem, own_sem, f_send, f_recv, a_send, a_recv, c_send, c_recv, r_send, r_recv, y_send, y_recv, z_send, z_recv,
-    g_send, g_recv, t_send, t_recv, b_send, b_recv,
+    pieces, rows_all, gram, group_in, y_in, z_in, whole, mat, ortho,
+    ham_sem, own_sem, f_send, f_recv, a_send, a_recv, r_send, r_recv, y_send, y_recv, z_send, z_recv,
+    g_send, g_recv, b_send, b_recv,
 ):
     bands, nodes = psi_ref.shape
     elems = conn_ref.shape[0]
@@ -196,8 +231,15 @@
     def z_peer(d):
         return {"space": (lax.rem(z + d, ZS) * YS + y) * CORES + core}
 
-    peers = [below, above, twin]
-    peers += [band_peer(d) for d in range(1, groups)]
+    def group_peer(c, d):
+        there = {"band": lax.rem(band + d, groups)}
+        if c > 0:
+            there["space"] = twin["space"]
+        return there
+
+    members = [(c, d) for c in range(CORES) for d in range(groups) if c + d > 0]
+    peers = [below, above]
+    peers += [group_peer(c, d) for c, d in members]
     peers += [y_peer(d) for d in range(1, YS)]
     peers += [z_peer(d) for d in range(1, ZS)]
     barrier = pltpu.get_barrier_semaphore()
@@ -365,25 +407,19 @@
     rows_all[mine, :] = pieces[band]
     finish(copies)
 
-    part = count // CORES
-    theirs = pl.ds(pl.multiple_of((1 - core) * part, 16), part)
-    ours = pl.ds(pl.multiple_of(core * part, 16), part)
-    gram[0] = nt(rows_all[theirs, :], rows_all[...])
-    copy = remote(gram.at[0], half_in, c_send.at[0], c_recv.at[0], twin)
-    copy.start()
-    gram[1] = nt(rows_all[ours, :], rows_all[...])
-    copy.wait()
-    half[...] = (gram[1] + half_in[...]).reshape(half.shape)
-
+    folded = fold(nt(rows_all[0:count, :], rows_all[...]))
+    for c in range(CORES):
+        gram[c] = folded[:, c * 128:(c + 1) * 128].reshape(gram.shape[1:])
     copies = []
-    for d in range(1, groups):
-        there = band_peer(d)
-        copies.append(remote(half.at[there["band"]], band_in.at[d - 1], r_send.at[d - 1], r_recv.at[d - 1], there))
+    for n, (c, d) in enumerate(members):
+        there = group_peer(c, d)
+        tile = gram.at[core if c == 0 else 1 - core, there["band"]]
+        copies.append(remote(tile, group_in.at[n], r_send.at[n], r_recv.at[n], there))
         copies[-1].start()
     finish(copies)
-    value = half[band]
-    for d in range(1, groups):
-        value = value + band_in[d - 1]
+    value = gram[core, band]
+    for n in range(len(members)):
+        value = value + group_in[n]
     y_in[y] = value
 
     copies = []
@@ -406,41 +442,58 @@
         value = value + z_in[k]
     whole[core, band] = value
 
-    copies = {}
+    copies = []
     piece = whole.at[core, band]
-    for d in range(1, groups):
-        copies[d] = remote(piece, piece, g_send.at[d - 1], g_recv.at[d - 1], band_peer(d))
-        copies[d].start()
-    forwarded = [remote(piece, piece, t_send.at[0], t_recv.at[0], twin)]
-    forwarded[0].start()
-    for d in sorted(copies, key=lambda d: (min(d, groups - d) not in (1, 3), d)):
-        copies[d].wait_recv()
-        piece = whole.at[core, lax.rem(band + groups - d, groups)]
-        forwarded.append(remote(piece, piece, t_send.at[d], t_recv.at[d], twin))
-        forwarded[-1].start()
-    for d in copies:
-        copies[d].wait_send()
-    finish(forwarded)
-
-    mat[...] = whole[...].reshape(count, wide) / total_nodes
-    factor_inverse(mat)
-    row = lax.broadcasted_iota(jnp.int32, (count, wide), 0)
-    column = lax.broadcasted_iota(jnp.int32, (count, wide), 1)
-    high, low = split(jnp.where(column <= row, mat[...], 0.0))
-    filtered = rows_all[...]
-    result = nn(high, filtered) + nn(low, filtered)
-    ortho[...] = result.astype(BF).reshape(ortho.shape)
-
-    copies = []
-    landing = out_ref.at[:, lanes(band * width, width)]
-    for d in range(1, groups):
-        there = band_peer(d)
-        copies.append(remote(ortho.at[there["band"]], landing, b_send.at[d - 1], b_recv.at[d - 1], there))
+    for n, (c, d) in enumerate(members):
+        copies.append(remote(piece, piece, g_send.at[n], g_recv.at[n], group_peer(c, d)))
         copies[-1].start()
-    copy = pltpu.make_async_copy(ortho.at[band], landing, own_sem)
-    copy.start()
-    copy.wait()
     finish(copies)
+
+    part = count // 2
+    folded = jnp.concatenate([whole[c].reshape(part, 128) for c in range(CORES)], axis=1) / total_nodes
+    mat[0:part, :], mat[part:, :] = unfold(folded)
+
+    def landing(source):
+        return out_ref.at[:, lanes(source * width, width)]
+
+    def back(k):
+        return remote(ortho.at[k], landing(band), b_send.at[k], b_recv.at[band], {"band": k})
+
+    def keep(k):
+        return pltpu.make_async_copy(ortho.at[k], landing(band), own_sem)
+
+    def rows_of(start, end):
+        value = mat[start:end, :]
+        row = start + lax.broadcasted_iota(jnp.int32, value.shape, 0)
+        column = lax.broadcasted_iota(jnp.int32, value.shape, 1)
+        parts = jnp.concatenate(split(jnp.where(column <= row, value, 0.0)), axis=0)
+        both = nn(parts, rows_all[...])
+        value = (both[0:end - start] + both[end - start:]).astype(BF)
+        ortho[start // bands:end // bands] = value.reshape((end - start) // bands, bands, width)
+
+    def deliver(start, end):
+        for k in range(start // bands, end // bands):
+            @pl.when(band != k)
+            def _():
+                back(k).start()
+
+            @pl.when(band == k)
+            def _():
+                keep(k).start()
+
+    panel = 2 * bands
+    factor_inverse(mat, panel, rows_of, deliver)
+    rows_of(count - panel, count)
+    deliver(count - panel, count)
+    for k in range(groups):
+        @pl.when(band != k)
+        def _():
+            back(k).wait_send()
+            remote(ortho.at[k], landing(k), b_send.at[k], b_recv.at[k], {"band": k}).wait_recv()
+
+        @pl.when(band == k)
+        def _():
+            keep(k).wait()
 
 
 def per_device(psi, ham, conn, face_rows):
@@ -456,7 +509,7 @@
     entries = elems * NODE_EL
     count = groups * bands
     wide = pl.cdiv(count, 128) * 128
-    unit = count // CORES // groups
+    unit = count // 2 // groups
     vmem = pl.BlockSpec(memory_space=pltpu.VMEM)
     anywhere = pl.BlockSpec(memory_space=pl.ANY)
     dma = pltpu.SemaphoreType.DMA
@@ -491,25 +544,21 @@
             pltpu.VMEM((bands, face_pad), F32),
             pltpu.VMEM((groups, bands, width), BF),
             pltpu.VMEM((wide, width), BF),
-            pltpu.VMEM((CORES, count // CORES, wide), F32),
-            pltpu.VMEM((count // CORES, wide), F32),
-            pltpu.VMEM((groups, unit, wide), F32),
-            pltpu.VMEM((groups - 1, unit, wide), F32),
-            pltpu.VMEM((YS, unit, wide), F32),
-            pltpu.VMEM((ZS, unit, wide), F32),
-            pltpu.VMEM((CORES, groups, unit, wide), F32),
+            pltpu.VMEM((CORES, groups, unit, 128), F32),
+            pltpu.VMEM((CORES * groups - 1, unit, 128), F32),
+            pltpu.VMEM((YS, unit, 128), F32),
+            pltpu.VMEM((ZS, unit, 128), F32),
+            pltpu.VMEM((CORES, groups, unit, 128), F32),
             pltpu.VMEM((count, wide), F32),
             pltpu.VMEM((groups, bands, width), BF),
             dma((HAM_PARTS,)), dma,
             dma((4,)), dma((4,)),
             dma((groups - 1,)), dma((groups - 1,)),
-            dma((1,)), dma((1,)),
-            dma((groups - 1,)), dma((groups - 1,)),
+            dma((CORES * groups - 1,)), dma((CORES * groups - 1,)),
             dma((YS - 1,)), dma((YS - 1,)),
             dma((ZS - 1,)), dma((ZS - 1,)),
-            dma((groups - 1,)), dma((groups - 1,)),
+            dma((CORES * groups - 1,)), dma((CORES * groups - 1,)),
             dma((groups,)), dma((groups,)),
-            dma((groups - 1,)), dma((groups - 1,)),
         ],
         compiler_params=pltpu.CompilerParams(
             collective_id=0, has_side_effects=True, vmem_limit_bytes=VMEM_LIMIT

time: 78.4 us -> 75 us (0.957)
  Pallas kernels: 75.4 us -> 72.6 us
    pallas_call x1, Pallas kernels: 75.4 us -> 72.6 us  [per_device(): pl.pallas_call(functools.partial(step_kernel, float(nodes * lax.axis_size...]
where the time goes in v3:
time: 75 us; the launch traced here: 74.2 us
  Pallas kernels  72.6 us (97%)
  other arithmetic  1.63 us (2%)
    pallas_call x1, Pallas kernels, per_device(): pl.pallas_call(functools.partial(step_kernel, float(nodes * lax.axis_size...  72.6 us
    convert_element_type x1, other arithmetic, per_device(): return result[:, 0:nodes].astype(F32)  1.63 us

profile of v3, /device:TPU:6, one launch (start us, length us, event | category | flops | bytes accessed | tf_op | source)
XLA Modules:
  0.0 74.2 jit_solution(8815649559798841109)
XLA Ops:
  0.0 72.6 %step.1 = bf16[16,4608]{1,0:T(8,128)(2,1)} custom-call(f32[16,4116]{1,0:T(8,128)} %psi_ref.1, bf16[12,512,512]{2,1,0:T(8,128)(2,1)} %ham_hbm.1, s32[12,512]{1,0:T(8,128)} %conn_ref.1, s32[588]{0:T(1024)} %face_ref.1), custom_call_target="tpu_custom_call" | custom-call | tf_op jit(solution)/shard_map/step/pallas_call | solution.py:517
  72.6 1.6 %slice_convert_fusion = f32[16,4116]{1,0:T(8,128)} fusion(bf16[16,4608]{1,0:T(8,128)(2,1)} %step.1), kind=kLoop, calls=%fused_computation | loop fusion | flops 65856 | bytes 395136 | tf_op jit(solution)/shard_map/convert_element_type | solution.py:568

commit v4 on v3

--- a/solution.py
+++ b/solution.py
@@ -64,10 +64,11 @@
 def place(parts, which, first, count, columns):
     zero = jnp.zeros_like(parts[0])
     keep = [which == first + h for h in range(count)]
-    rows = [jnp.where(k, part, zero) for part in parts for k in keep]
-    result = nt(jnp.concatenate(rows, axis=0), columns)
-    size = result.shape[0] // len(parts)
-    return sum(result[n * size:(n + 1) * size] for n in range(1, len(parts))) + result[0:size]
+    total = None
+    for part in parts:
+        value = nt(jnp.concatenate([jnp.where(k, part, zero) for k in keep], axis=0), columns)
+        total = value if total is None else total + value
+    return total
 
 
 def indicator(low, depth):
@@ -194,12 +195,12 @@
 
 
 def step_kernel(
-    total_nodes, psi_ref, ham_hbm, conn_ref, face_ref, out_ref,
-    ham, onehot, onehot_ghost, onehot_face, hi_ref, hi_ghost, hi_face, base, field, xb, xg,
-    gathered, high_ref, low_ref,
+    total_nodes, psi_hbm, ham_hbm, conn_hbm, face_hbm, out_ref,
+    psi_ref, conn_ref, face_ref, ham, onehot, onehot_ghost, onehot_face, hi_ref, hi_ghost, hi_face, base, field, xb, xg,
+    gathered, ghosted, products, high_ref, low_ref, tail_high, tail_low, kept,
     send1, send2, send3, send4, got1, got2, got3, got4,
     pieces, rows_all, gram, group_in, y_in, z_in, whole, mat, ortho,
-    ham_sem, own_sem, f_send, f_recv, a_send, a_recv, r_send, r_recv, y_send, y_recv, z_send, z_recv,
+    in_sem, ham_sem, own_sem, f_send, f_recv, a_send, a_recv, r_send, r_recv, y_send, y_recv, z_send, z_recv,
     g_send, g_recv, b_send, b_recv,
 ):
     bands, nodes = psi_ref.shape
@@ -222,6 +223,13 @@
     above = {"space": lax.rem(space + 1, domains)}
     twin = {"space": space + 1 - 2 * core}
 
+    inputs = [
+        pltpu.make_async_copy(source, held, in_sem.at[n])
+        for n, (source, held) in enumerate([(face_hbm, face_ref), (psi_hbm, psi_ref), (conn_hbm, conn_ref)])
+    ]
+    for c in inputs:
+        c.start()
+
     def band_peer(d):
         return {"band": lax.rem(band + d, groups)}
 
@@ -253,17 +261,7 @@
         ham_copies.append(pltpu.make_async_copy(ham_hbm.at[part], ham.at[part], ham_sem.at[k]))
         ham_copies[-1].start()
 
-    for h in range(own_blocks):
-        rows = slice(h * bands, (h + 1) * bands)
-        if (h + 1) * LO <= nodes:
-            value = psi_ref[:, h * LO:(h + 1) * LO]
-            base[rows, :] = value
-            xb[rows, :] = value.astype(BF)
-        else:
-            base[rows, :] = jnp.zeros((bands, LO), F32)
-            base[rows, 0:nodes - h * LO] = psi_ref[:, h * LO:nodes]
-            xb[rows, :] = base[rows, :].astype(BF)
-
+    inputs[0].wait()
     depth = lax.broadcasted_iota(jnp.int32, (LO, NODE_EL), 0).astype(F32).astype(BF)
     for k in range(face_pad // 128):
         size = min(128, faces - k * 128)
@@ -282,11 +280,23 @@
         table = nn(blocks, onehot_face[...]).astype(BF)
         return pick(table, hi_face[...], 0, own_blocks, jnp.zeros((bands, face_pad), BF))
 
+    inputs[1].wait()
+    for h in range(own_blocks):
+        rows = slice(h * bands, (h + 1) * bands)
+        if (h + 1) * LO <= nodes:
+            value = psi_ref[:, h * LO:(h + 1) * LO]
+            base[rows, :] = value
+            xb[rows, :] = value.astype(BF)
+        else:
+            base[rows, :] = jnp.zeros((bands, LO), F32)
+            base[rows, 0:nodes - h * LO] = psi_ref[:, h * LO:nodes]
+            xb[rows, :] = base[rows, :].astype(BF)
     send1[...] = take_face(xb[...])
     pl.semaphore_wait(barrier, len(peers))
     copy1 = remote(send1, got1, f_send.at[0], f_recv.at[0], below)
     copy1.start()
 
+    inputs[2].wait()
     spot = lax.broadcasted_iota(jnp.int32, (1, NODE_EL), 1)
 
     def prepare(e, carry):
@@ -320,66 +330,79 @@
             size = min(LO, face_pad - h * LO)
             xg[h * bands:(h + 1) * bands, 0:size] = values[:, h * LO:h * LO + size].astype(BF)
         table = nn(xg[...], onehot_ghost[...]).astype(BF)
-        found = pick(table, hi_ghost[...], own_blocks, ghost_blocks, jnp.zeros((bands, elems * TAIL), BF))
-        for e in range(elems):
-            cols = slice((e + 1) * NODE_EL - TAIL, (e + 1) * NODE_EL)
-            gathered[:, cols] = gathered[:, cols] + found[:, e * TAIL:(e + 1) * TAIL]
-
-    def multiply():
+        ghosted[...] = pick(table, hi_ghost[...], own_blocks, ghost_blocks, jnp.zeros((bands, elems * TAIL), BF))
+
+    def multiply_own():
         def body(e, carry):
             cols = lanes(e * NODE_EL, NODE_EL)
-            high_ref[:, cols], low_ref[:, cols] = split(nn(gathered[:, cols], ham[e]))
+            products[:, cols] = nn(gathered[:, cols], ham[e])
             return carry
 
         lax.fori_loop(0, elems, body, 0, unroll=4)
 
     def upper():
-        cols = [slice((e + 1) * NODE_EL - TAIL, (e + 1) * NODE_EL) for e in range(elems)]
-        high = jnp.concatenate([high_ref[:, c] for c in cols], axis=1)
-        low = jnp.concatenate([low_ref[:, c] for c in cols], axis=1)
-        total = place([high, low], hi_ghost[...], own_blocks, ghost_blocks, onehot_ghost[...])
+        for e in range(elems):
+            some = slice(e * TAIL, (e + 1) * TAIL)
+            cols = slice((e + 1) * NODE_EL - TAIL, (e + 1) * NODE_EL)
+            value = products[:, cols] + nn(ghosted[:, some], ham[e, NODE_EL - TAIL:, NODE_EL - TAIL:])
+            high, low = split(value)
+            tail_high[:, some], tail_low[:, some] = high, low
+            high_ref[:, cols], low_ref[:, cols] = high, low
+        total = place([tail_high[...], tail_low[...]], hi_ghost[...], own_blocks, ghost_blocks, onehot_ghost[...])
         parts = [
             total[h * bands:(h + 1) * bands, 0:min(LO, face_pad - h * LO)] for h in range(ghost_blocks)
         ]
         return jnp.concatenate(parts, axis=1)
 
+    def multiply_ghost():
+        def body(e, carry):
+            some = lanes(e * TAIL, TAIL)
+            cols = lanes(e * NODE_EL, NODE_EL - TAIL)
+            value = products[:, cols] + nn(ghosted[:, some], ham[e, NODE_EL - TAIL:, 0:NODE_EL - TAIL])
+            high_ref[:, cols], low_ref[:, cols] = split(value)
+            return carry
+
+        lax.fori_loop(0, elems, body, 0, unroll=4)
+
     def scatter_own():
-        half_cols = elems * NODE_EL // 2
+        size = elems * NODE_EL // 4
         total = None
-        for k in range(2):
-            cols = slice(k * half_cols, (k + 1) * half_cols)
+        for k in range(4):
+            cols = slice(k * size, (k + 1) * size)
             value = place([high_ref[:, cols], low_ref[:, cols]], hi_ref[:, cols], 0, own_blocks, onehot[:, cols])
             total = value if total is None else total + value
         return total
 
     def put_face(received):
-        return place(list(split(received)), hi_face[...], 0, own_blocks, onehot_face[...])
+        return place([received], hi_face[...], 0, own_blocks, onehot_face[...])
 
     gather_own()
+    for c in ham_copies:
+        c.wait()
+    multiply_own()
     copy1.wait()
     gather_ghost(got1[...])
-    for c in ham_copies:
-        c.wait()
-    multiply()
-    send2[...] = upper()
+    kept[...] = upper()
+    send2[...] = kept[...].astype(BF)
     copy2 = remote(send2, got2, f_send.at[1], f_recv.at[1], above)
     copy2.start()
+    multiply_ghost()
     partial_value = (scatter_own() - CENTER * base[...]) / HALF_WIDTH
     field[...] = partial_value
-    high, low = split(partial_value)
-    send3[...] = take_face(high).astype(F32) + take_face(low).astype(F32)
+    send3[...] = take_face(partial_value.astype(BF))
     copy3 = remote(send3, got3, f_send.at[2], f_recv.at[2], below)
     copy3.start()
     copy2.wait()
-    field[...] += put_face(got2[...] / HALF_WIDTH)
+    field[...] += put_face(got2[...]) / HALF_WIDTH
     xb[...] = field[...].astype(BF)
     gather_own()
+    multiply_own()
     copy3.wait()
-    gather_ghost(got3[...] + send2[...] / HALF_WIDTH)
-    multiply()
-    send4[...] = upper()
+    gather_ghost(got3[...].astype(F32) + kept[...] / HALF_WIDTH)
+    send4[...] = upper().astype(BF)
     copy4 = remote(send4, got4, f_send.at[3], f_recv.at[3], above)
     copy4.start()
+    multiply_ghost()
     partial_value = scatter_own() - CENTER * field[...]
     copy4.wait()
     field[...] = 2.0 * ((partial_value + put_face(got4[...])) / HALF_WIDTH) - base[...]
@@ -510,16 +533,18 @@
     count = groups * bands
     wide = pl.cdiv(count, 128) * 128
     unit = count // 2 // groups
-    vmem = pl.BlockSpec(memory_space=pltpu.VMEM)
     anywhere = pl.BlockSpec(memory_space=pl.ANY)
     dma = pltpu.SemaphoreType.DMA
 
     result = pl.pallas_call(
         functools.partial(step_kernel, float(nodes * lax.axis_size("space"))),
         out_shape=jax.ShapeDtypeStruct((bands, groups * width), BF),
-        in_specs=[vmem, anywhere, vmem, vmem],
+        in_specs=[anywhere] * 4,
         out_specs=anywhere,
         scratch_shapes=[
+            pltpu.VMEM(psi.shape, F32),
+            pltpu.VMEM(conn.shape, jnp.int32),
+            pltpu.VMEM(face_rows.shape, jnp.int32),
             pltpu.VMEM(ham.shape, BF),
             pltpu.VMEM((LO, entries), BF),
             pltpu.VMEM((LO, elems * TAIL), BF),
@@ -532,16 +557,21 @@
             pltpu.VMEM((own, LO), BF),
             pltpu.VMEM((ghost_blocks * bands, LO), BF),
             pltpu.VMEM((bands, entries), BF),
+            pltpu.VMEM((bands, elems * TAIL), BF),
+            pltpu.VMEM((bands, entries), F32),
             pltpu.VMEM((bands, entries), BF),
             pltpu.VMEM((bands, entries), BF),
-            pltpu.VMEM((bands, face_pad), BF),
+            pltpu.VMEM((bands, elems * TAIL), BF),
+            pltpu.VMEM((bands, elems * TAIL), BF),
             pltpu.VMEM((bands, face_pad), F32),
-            pltpu.VMEM((bands, face_pad), F32),
-            pltpu.VMEM((bands, face_pad), F32),
-            pltpu.VMEM((bands, face_pad), BF),
-            pltpu.VMEM((bands, face_pad), F32),
-            pltpu.VMEM((bands, face_pad), F32),
-            pltpu.VMEM((bands, face_pad), F32),
+            pltpu.VMEM((bands, face_pad), BF),
+            pltpu.VMEM((bands, face_pad), BF),
+            pltpu.VMEM((bands, face_pad), BF),
+            pltpu.VMEM((bands, face_pad), BF),
+            pltpu.VMEM((bands, face_pad), BF),
+            pltpu.VMEM((bands, face_pad), BF),
+            pltpu.VMEM((bands, face_pad), BF),
+            pltpu.VMEM((bands, face_pad), BF),
             pltpu.VMEM((groups, bands, width), BF),
             pltpu.VMEM((wide, width), BF),
             pltpu.VMEM((CORES, groups, unit, 128), F32),
@@ -551,7 +581,7 @@
             pltpu.VMEM((CORES, groups, unit, 128), F32),
             pltpu.VMEM((count, wide), F32),
             pltpu.VMEM((groups, bands, width), BF),
-            dma((HAM_PARTS,)), dma,
+            dma((3,)), dma((HAM_PARTS,)), dma,
             dma((4,)), dma((4,)),
             dma((groups - 1,)), dma((groups - 1,)),
             dma((CORES * groups - 1,)), dma((CORES * groups - 1,)),

time: 75 us -> 71.7 us (0.956)
  Pallas kernels: 72.6 us -> 70 us
    pallas_call x1, Pallas kernels: 72.6 us -> 70 us  [per_device(): pl.pallas_call(functools.partial(step_kernel, float(nodes * lax.axis_size...]
where the time goes in v4:
time: 71.7 us; the launch traced here: 71.6 us
  Pallas kernels  70 us (98%)
  other arithmetic  1.63 us (2%)
    pallas_call x1, Pallas kernels, per_device(): pl.pallas_call(functools.partial(step_kernel, float(nodes * lax.axis_size...  70 us
    convert_element_type x1, other arithmetic, per_device(): return result[:, 0:nodes].astype(F32)  1.63 us

profile of v4, /device:TPU:6, one launch (start us, length us, event | category | flops | bytes accessed | tf_op | source)
XLA Modules:
  0.0 71.6 jit_solution(17366241745421451056)
XLA Ops:
  0.0 70.0 %step.1 = bf16[16,4608]{1,0:T(8,128)(2,1)} custom-call(f32[16,4116]{1,0:T(8,128)} %psi_hbm.1, bf16[12,512,512]{2,1,0:T(8,128)(2,1)} %ham_hbm.1, s32[12,512]{1,0:T(8,128)} %conn_hbm.1, s32[588]{0:T(1024)} %face_hbm.1), custom_call_target="tpu_custom_call" | custom-call | tf_op jit(solution)/shard_map/step/pallas_call | solution.py:539
  70.0 1.6 %slice_convert_fusion = f32[16,4116]{1,0:T(8,128)} fusion(bf16[16,4608]{1,0:T(8,128)(2,1)} %step.1), kind=kLoop, calls=%fused_computation | loop fusion | flops 65856 | bytes 395136 | tf_op jit(solution)/shard_map/convert_element_type | solution.py:598

commit v5 on v4

--- a/solution.py
+++ b/solution.py
@@ -18,7 +18,7 @@
 F32 = jnp.float32
 VMEM_LIMIT = 60 * 1024 * 1024
 
-CORES, YS, ZS = 2, 8, 4
+CORES, YS, ZS, BAND_Z = 2, 8, 4, 3
 HAM_PARTS = 4
 NT = (((1,), (1,)), ((), ()))
 TN = (((0,), (0,)), ((), ()))
@@ -164,34 +164,22 @@
 
 
 def fold(matrix):
-    half = matrix.shape[0] // 2
-    upper, lower = matrix[0:half, :], matrix[half:, :]
-    row = lax.broadcasted_iota(jnp.int32, lower.shape, 0)
-    lane = lax.broadcasted_iota(jnp.int32, lower.shape, 1)
-    diagonal = jnp.sum(jnp.where(lane == row + half, lower, 0.0), axis=1, keepdims=True)
-    mixed = jnp.where((lane >= half) & (lane - half <= row), pltpu.roll(upper, half, 1), lower)
-    return jnp.where(lane < 2 * half, mixed, diagonal)
+    rest = matrix.shape[0] - 128
+    corner = pltpu.roll(matrix[128:, 128:], rest, 1)
+    lane = lax.broadcasted_iota(jnp.int32, corner.shape, 1)
+    first = jnp.where(lane < rest, matrix[0:rest, 0:128], corner)
+    return jnp.concatenate([first, matrix[rest:, 0:128]], axis=0)
 
 
 def unfold(folded):
-    half, wide = folded.shape
-    row = lax.broadcasted_iota(jnp.int32, folded.shape, 0)
+    count = folded.shape[0]
+    rest = count - 128
+    turned = pltpu.roll(folded[rest:, :].T, rest, 1)
     lane = lax.broadcasted_iota(jnp.int32, folded.shape, 1)
-    diagonal = jnp.broadcast_to(folded[:, 2 * half:2 * half + 1], folded.shape)
-    mixed = pltpu.roll(folded, wide - half, 1)
-    zeros = jnp.zeros((128 - half, 128), F32)
-
-    def flip(value):
-        square = jnp.concatenate([value[:, 0:128], zeros], axis=0).T[0:half, :]
-        return jnp.concatenate([square, jnp.zeros((half, wide - 128), F32)], axis=1)
-
-    other = flip(jnp.where(lane < half, mixed, 0.0))
-    corner = flip(jnp.where(lane < half, folded, 0.0))
-    first = jnp.where(lane < half, jnp.where(lane <= row, mixed, other), pltpu.roll(corner, half, 1))
-    last = jnp.where(lane == row, diagonal, jnp.where(lane > row, mixed, other))
-    last = jnp.where(lane < half, folded, pltpu.roll(last, half, 1))
-    inside = lane < 2 * half
-    return jnp.where(inside, first, 0.0), jnp.where(inside, last, 0.0)
+    first = jnp.where(lane[0:rest] < rest, folded[0:rest, :], turned[0:rest, :])
+    left = jnp.concatenate([first, folded[rest:, :]], axis=0)
+    right = jnp.concatenate([turned, pltpu.roll(folded[0:rest, :], rest, 1)], axis=0)
+    return jnp.concatenate([left, jnp.where(lane < rest, right, 0.0)], axis=1)
 
 
 def step_kernel(
@@ -230,8 +218,16 @@
     for c in inputs:
         c.start()
 
-    def band_peer(d):
-        return {"band": lax.rem(band + d, groups)}
+    band_x = groups // BAND_Z
+    steps = [(i, k) for i in range(band_x) for k in range(BAND_Z) if i + k > 0]
+    steps.sort(key=lambda step: -(min(step[0], band_x - step[0]) + 1.5 * (step[1] > 0)))
+
+    def band_at(step):
+        i, k = step
+        return lax.rem(band // BAND_Z + i, band_x) * BAND_Z + lax.rem(lax.rem(band, BAND_Z) + k, BAND_Z)
+
+    def band_peer(step):
+        return {"band": band_at(step)}
 
     def y_peer(d):
         return {"space": (z * YS + lax.rem(y + d, YS)) * CORES + core}
@@ -239,17 +235,19 @@
     def z_peer(d):
         return {"space": (lax.rem(z + d, ZS) * YS + y) * CORES + core}
 
-    def group_peer(c, d):
-        there = {"band": lax.rem(band + d, groups)}
+    def group_peer(c, step):
+        there = {"band": band_at(step)}
         if c > 0:
             there["space"] = twin["space"]
         return there
 
-    members = [(c, d) for c in range(CORES) for d in range(groups) if c + d > 0]
+    members = [(c, step) for step in steps for c in range(CORES)] + [(1, (0, 0))]
+    y_steps = sorted(range(1, YS), key=lambda d: -min(d, YS - d))
+    z_steps = sorted(range(1, ZS), key=lambda d: -min(d, ZS - d))
     peers = [below, above]
     peers += [group_peer(c, d) for c, d in members]
-    peers += [y_peer(d) for d in range(1, YS)]
-    peers += [z_peer(d) for d in range(1, ZS)]
+    peers += [y_peer(d) for d in y_steps]
+    peers += [z_peer(d) for d in z_steps]
     barrier = pltpu.get_barrier_semaphore()
     for there in peers:
         pl.semaphore_signal(barrier, inc=1, device_id=there, device_id_type=MESH)
@@ -423,16 +421,15 @@
 
     mine = pl.ds(pl.multiple_of(band * bands, bands), bands)
     copies = []
-    for d in range(1, groups):
-        there = band_peer(d)
-        copies.append(remote(pieces.at[there["band"]], rows_all.at[mine], a_send.at[d - 1], a_recv.at[d - 1], there))
+    for n, step in enumerate(steps):
+        there = band_peer(step)
+        copies.append(remote(pieces.at[there["band"]], rows_all.at[mine], a_send.at[n], a_recv.at[n], there))
         copies[-1].start()
     rows_all[mine, :] = pieces[band]
     finish(copies)
 
     folded = fold(nt(rows_all[0:count, :], rows_all[...]))
-    for c in range(CORES):
-        gram[c] = folded[:, c * 128:(c + 1) * 128].reshape(gram.shape[1:])
+    gram[...] = folded.reshape(gram.shape)
     copies = []
     for n, (c, d) in enumerate(members):
         there = group_peer(c, d)
@@ -446,7 +443,7 @@
     y_in[y] = value
 
     copies = []
-    for d in range(1, YS):
+    for d in y_steps:
         copies.append(remote(y_in.at[y], y_in.at[y], y_send.at[d - 1], y_recv.at[d - 1], y_peer(d)))
         copies[-1].start()
     finish(copies)
@@ -456,7 +453,7 @@
     z_in[z] = value
 
     copies = []
-    for d in range(1, ZS):
+    for d in z_steps:
         copies.append(remote(z_in.at[z], z_in.at[z], z_send.at[d - 1], z_recv.at[d - 1], z_peer(d)))
         copies[-1].start()
     finish(copies)
@@ -472,9 +469,7 @@
         copies[-1].start()
     finish(copies)
 
-    part = count // 2
-    folded = jnp.concatenate([whole[c].reshape(part, 128) for c in range(CORES)], axis=1) / total_nodes
-    mat[0:part, :], mat[part:, :] = unfold(folded)
+    mat[...] = unfold(whole[...].reshape(count, 128) / total_nodes)
 
     def landing(source):
         return out_ref.at[:, lanes(source * width, width)]
@@ -538,9 +533,9 @@
 
     result = pl.pallas_call(
         functools.partial(step_kernel, float(nodes * lax.axis_size("space"))),
-        out_shape=jax.ShapeDtypeStruct((bands, groups * width), BF),
+        out_shape=pltpu.VMEM((bands, groups * width), BF),
         in_specs=[anywhere] * 4,
-        out_specs=anywhere,
+        out_specs=pl.BlockSpec(memory_space=pltpu.VMEM),
         scratch_shapes=[
             pltpu.VMEM(psi.shape, F32),
             pltpu.VMEM(conn.shape, jnp.int32),

time: 71.7 us -> 70.5 us (0.983)
  other arithmetic: 1.63 us -> 0.72 us
  Pallas kernels: 70 us -> 69.2 us
    convert_element_type x1, other arithmetic: 1.63 us -> 0.72 us  [per_device(): return result[:, 0:nodes].astype(F32)]
    pallas_call x1, Pallas kernels: 70 us -> 69.2 us  [per_device(): pl.pallas_call(functools.partial(step_kernel, float(nodes * lax.axis_size...]
where the time goes in v5:
time: 70.5 us; the launch traced here: 69.9 us
  Pallas kernels  69.2 us (98%)
  other arithmetic  0.72 us (1%)
    pallas_call x1, Pallas kernels, per_device(): pl.pallas_call(functools.partial(step_kernel, float(nodes * lax.axis_size...  69.2 us

profile of v5, /device:TPU:6, one launch (start us, length us, event | category | flops | bytes accessed | tf_op | source)
XLA Modules:
  0.0 69.9 jit_solution(14996929177311980297)
XLA Ops:
  0.0 69.2 %step.1 = bf16[16,4608]{1,0:T(8,128)(2,1)S(1)} custom-call(f32[16,4116]{1,0:T(8,128)} %psi_hbm.1, bf16[12,512,512]{2,1,0:T(8,128)(2,1)} %ham_hbm.1, s32[12,512]{1,0:T(8,128)} %conn_hbm.1, s32[588]{0:T(1024)} %face_hbm.1), custom_call_target="tpu_custom_call" | custom-call | tf_op jit(solution)/shard_map/step/pallas_call | solution.py:534
  69.2 0.7 %slice_convert_fusion = f32[16,4116]{1,0:T(8,128)} fusion(bf16[16,4608]{1,0:T(8,128)(2,1)S(1)} %step.1), kind=kLoop, calls=%fused_computation | loop fusion | flops 65856 | bytes 395136 | tf_op jit(solution)/shard_map/convert_element_type | solution.py:593

commit v6 on v5

--- a/solution.py
+++ b/solution.py
@@ -61,14 +61,10 @@
     return total
 
 
-def place(parts, which, first, count, columns):
-    zero = jnp.zeros_like(parts[0])
-    keep = [which == first + h for h in range(count)]
-    total = None
-    for part in parts:
-        value = nt(jnp.concatenate([jnp.where(k, part, zero) for k in keep], axis=0), columns)
-        total = value if total is None else total + value
-    return total
+def place(part, which, first, count, columns):
+    zero = jnp.zeros_like(part)
+    rows = [jnp.where(which == first + h, part, zero) for h in range(count)]
+    return nt(jnp.concatenate(rows, axis=0), columns)
 
 
 def indicator(low, depth):
@@ -185,7 +181,7 @@
 def step_kernel(
     total_nodes, psi_hbm, ham_hbm, conn_hbm, face_hbm, out_ref,
     psi_ref, conn_ref, face_ref, ham, onehot, onehot_ghost, onehot_face, hi_ref, hi_ghost, hi_face, base, field, xb, xg,
-    gathered, ghosted, products, high_ref, low_ref, tail_high, tail_low, kept,
+    gathered, ghosted, products, high_ref, low_ref, tail_high, kept,
     send1, send2, send3, send4, got1, got2, got3, got4,
     pieces, rows_all, gram, group_in, y_in, z_in, whole, mat, ortho,
     in_sem, ham_sem, own_sem, f_send, f_recv, a_send, a_recv, r_send, r_recv, y_send, y_recv, z_send, z_recv,
@@ -321,7 +317,7 @@
             gathered[:, cols] = pick(table, hi_ref[:, cols], 0, own_blocks, jnp.zeros((bands, NODE_EL), BF))
             return carry
 
-        lax.fori_loop(0, elems, body, 0, unroll=4)
+        lax.fori_loop(0, elems, body, 0, unroll=12)
 
     def gather_ghost(values):
         for h in range(ghost_blocks):
@@ -338,15 +334,23 @@
 
         lax.fori_loop(0, elems, body, 0, unroll=4)
 
+    def tail_cols(e):
+        return slice((e + 1) * NODE_EL - TAIL, (e + 1) * NODE_EL)
+
+    def multiply_tail():
+        for e in range(elems):
+            cols = slice(e * NODE_EL, (e + 1) * NODE_EL)
+            products[:, tail_cols(e)] = nn(gathered[:, cols], ham[e, :, NODE_EL - TAIL:])
+
     def upper():
         for e in range(elems):
             some = slice(e * TAIL, (e + 1) * TAIL)
-            cols = slice((e + 1) * NODE_EL - TAIL, (e + 1) * NODE_EL)
+            cols = tail_cols(e)
             value = products[:, cols] + nn(ghosted[:, some], ham[e, NODE_EL - TAIL:, NODE_EL - TAIL:])
             high, low = split(value)
-            tail_high[:, some], tail_low[:, some] = high, low
+            tail_high[:, some] = high
             high_ref[:, cols], low_ref[:, cols] = high, low
-        total = place([tail_high[...], tail_low[...]], hi_ghost[...], own_blocks, ghost_blocks, onehot_ghost[...])
+        total = place(tail_high[...], hi_ghost[...], own_blocks, ghost_blocks, onehot_ghost[...])
         parts = [
             total[h * bands:(h + 1) * bands, 0:min(LO, face_pad - h * LO)] for h in range(ghost_blocks)
         ]
@@ -362,17 +366,29 @@
 
         lax.fori_loop(0, elems, body, 0, unroll=4)
 
-    def scatter_own():
+    def multiply_rest():
+        for e in range(elems):
+            gathered[:, tail_cols(e)] = gathered[:, tail_cols(e)] + ghosted[:, e * TAIL:(e + 1) * TAIL]
+
+        def body(e, carry):
+            cols = lanes(e * NODE_EL, NODE_EL - TAIL)
+            value = nn(gathered[:, lanes(e * NODE_EL, NODE_EL)], ham[e, :, 0:NODE_EL - TAIL])
+            high_ref[:, cols], low_ref[:, cols] = split(value)
+            return carry
+
+        lax.fori_loop(0, elems, body, 0, unroll=4)
+
+    def scatter_own(part):
         size = elems * NODE_EL // 4
         total = None
         for k in range(4):
             cols = slice(k * size, (k + 1) * size)
-            value = place([high_ref[:, cols], low_ref[:, cols]], hi_ref[:, cols], 0, own_blocks, onehot[:, cols])
+            value = place(part[:, cols], hi_ref[:, cols], 0, own_blocks, onehot[:, cols])
             total = value if total is None else total + value
         return total
 
     def put_face(received):
-        return place([received], hi_face[...], 0, own_blocks, onehot_face[...])
+        return place(received, hi_face[...], 0, own_blocks, onehot_face[...])
 
     gather_own()
     for c in ham_copies:
@@ -385,23 +401,24 @@
     copy2 = remote(send2, got2, f_send.at[1], f_recv.at[1], above)
     copy2.start()
     multiply_ghost()
-    partial_value = (scatter_own() - CENTER * base[...]) / HALF_WIDTH
+    partial_value = scatter_own(high_ref) - CENTER * base[...]
     field[...] = partial_value
-    send3[...] = take_face(partial_value.astype(BF))
+    send3[...] = take_face((partial_value / HALF_WIDTH).astype(BF))
     copy3 = remote(send3, got3, f_send.at[2], f_recv.at[2], below)
     copy3.start()
+    field[...] += scatter_own(low_ref)
     copy2.wait()
-    field[...] += put_face(got2[...]) / HALF_WIDTH
+    field[...] = (field[...] + put_face(got2[...])) / HALF_WIDTH
     xb[...] = field[...].astype(BF)
     gather_own()
-    multiply_own()
+    multiply_tail()
     copy3.wait()
     gather_ghost(got3[...].astype(F32) + kept[...] / HALF_WIDTH)
     send4[...] = upper().astype(BF)
     copy4 = remote(send4, got4, f_send.at[3], f_recv.at[3], above)
     copy4.start()
-    multiply_ghost()
-    partial_value = scatter_own() - CENTER * field[...]
+    multiply_rest()
+    partial_value = scatter_own(high_ref) + scatter_own(low_ref) - CENTER * field[...]
     copy4.wait()
     field[...] = 2.0 * ((partial_value + put_face(got4[...])) / HALF_WIDTH) - base[...]
 
@@ -556,7 +573,6 @@
             pltpu.VMEM((bands, entries), F32),
             pltpu.VMEM((bands, entries), BF),
             pltpu.VMEM((bands, entries), BF),
-            pltpu.VMEM((bands, elems * TAIL), BF),
             pltpu.VMEM((bands, elems * TAIL), BF),
             pltpu.VMEM((bands, face_pad), F32),
             pltpu.VMEM((bands, face_pad), BF),

time: 70.5 us -> 70.3 us (level)
  no operation moved by 1% of the time
where the time goes in v6:
time: 70.3 us; the launch traced here: 70 us
  Pallas kernels  69.3 us (99%)
  other arithmetic  0.72 us (1%)
    pallas_call x1, Pallas kernels, per_device(): pl.pallas_call(functools.partial(step_kernel, float(nodes * lax.axis_size...  69.3 us

profile of v6, /device:TPU:6, one launch (start us, length us, event | category | flops | bytes accessed | tf_op | source)
XLA Modules:
  0.0 70.0 jit_solution(18241006544612347554)
XLA Ops:
  0.0 69.3 %step.1 = bf16[16,4608]{1,0:T(8,128)(2,1)S(1)} custom-call(f32[16,4116]{1,0:T(8,128)} %psi_hbm.1, bf16[12,512,512]{2,1,0:T(8,128)(2,1)} %ham_hbm.1, s32[12,512]{1,0:T(8,128)} %conn_hbm.1, s32[588]{0:T(1024)} %face_hbm.1), custom_call_target="tpu_custom_call" | custom-call | tf_op jit(solution)/shard_map/step/pallas_call | solution.py:551
  69.3 0.7 %slice_convert_fusion = f32[16,4116]{1,0:T(8,128)} fusion(bf16[16,4608]{1,0:T(8,128)(2,1)S(1)} %step.1), kind=kLoop, calls=%fused_computation | loop fusion | flops 65856 | bytes 395136 | tf_op jit(solution)/shard_map/convert_element_type | solution.py:609

commit v7 on v6

--- a/solution.py
+++ b/solution.py
@@ -76,7 +76,7 @@
     return jnp.broadcast_to(value.astype(F32), (rows, value.shape[1])).astype(BF)
 
 
-def factor_inverse(mat, panel, beside, after):
+def factor_inverse(mat, tops, beside, after):
     size, wide = mat.shape
     step = 8
     lane = lax.broadcasted_iota(jnp.int32, (step, 128), 1)
@@ -89,10 +89,10 @@
     def spread_row(value, i):
         return jnp.broadcast_to(value[i:i + 1, :], (step, 128))
 
-    for top in range(0, size, panel):
-        if top > 0:
-            beside(top - panel, top)
-        groups = min(panel, size - top) // step
+    for number, top in enumerate(tops):
+        if number > 0:
+            beside(tops[number - 1], top)
+        groups = (tops[number + 1] - top if number + 1 < len(tops) else size - top) // step
         block = [
             [mat[top + step * g:top + step * (g + 1), t * 128:(t + 1) * 128] for t in tiles] for g in range(groups)
         ]
@@ -155,8 +155,8 @@
             column = lax.broadcasted_iota(jnp.int32, rest.shape, 1)
             rest = jnp.where((column >= top) & (column < end), 0.0, rest)
             mat[end:size, :] = rest - update[end - first:size - first, :]
-        if top > 0:
-            after(top - panel, top)
+        if number > 0:
+            after(tops[number - 1], top)
 
 
 def fold(matrix):
@@ -516,10 +516,10 @@
             def _():
                 keep(k).start()
 
-    panel = 2 * bands
-    factor_inverse(mat, panel, rows_of, deliver)
-    rows_of(count - panel, count)
-    deliver(count - panel, count)
+    tops = list(range(0, count, 2 * bands)) + [count - bands]
+    factor_inverse(mat, tops, rows_of, deliver)
+    rows_of(tops[-1], count)
+    deliver(tops[-1], count)
     for k in range(groups):
         @pl.when(band != k)
         def _():

time: 70.3 us -> 70 us (level)
  no operation moved by 1% of the time
where the time goes in v7:
time: 70 us; the launch traced here: 69.8 us
  Pallas kernels  69 us (99%)
  other arithmetic  0.72 us (1%)
    pallas_call x1, Pallas kernels, per_device(): pl.pallas_call(functools.partial(step_kernel, float(nodes * lax.axis_size...  69 us

profile of v7, /device:TPU:6, one launch (start us, length us, event | category | flops | bytes accessed | tf_op | source)
XLA Modules:
  0.0 69.8 jit_solution(6867862283063256074)
XLA Ops:
  0.0 69.0 %step.1 = bf16[16,4608]{1,0:T(8,128)(2,1)S(1)} custom-call(f32[16,4116]{1,0:T(8,128)} %psi_hbm.1, bf16[12,512,512]{2,1,0:T(8,128)(2,1)} %ham_hbm.1, s32[12,512]{1,0:T(8,128)} %conn_hbm.1, s32[588]{0:T(1024)} %face_hbm.1), custom_call_target="tpu_custom_call" | custom-call | tf_op jit(solution)/shard_map/step/pallas_call | solution.py:551
  69.0 0.7 %slice_convert_fusion = f32[16,4116]{1,0:T(8,128)} fusion(bf16[16,4608]{1,0:T(8,128)(2,1)S(1)} %step.1), kind=kLoop, calls=%fused_computation | loop fusion | flops 65856 | bytes 395136 | tf_op jit(solution)/shard_map/convert_element_type | solution.py:609

commit v8 on v6

--- a/solution.py
+++ b/solution.py
@@ -87,7 +87,7 @@
         return jnp.broadcast_to(value[:, j:j + 1], (step, 128))
 
     def spread_row(value, i):
-        return jnp.broadcast_to(value[i:i + 1, :], (step, 128))
+        return jnp.take_along_axis(value, jnp.full((step, 128), i, jnp.int32), axis=0)
 
     for top in range(0, size, panel):
         if top > 0:

time: 70.3 us -> 69 us (0.982)
  Pallas kernels: 69.3 us -> 68.1 us
    pallas_call x1, Pallas kernels: 69.3 us -> 68.1 us  [per_device(): pl.pallas_call(functools.partial(step_kernel, float(nodes * lax.axis_size...]
where the time goes in v8:
time: 69 us; the launch traced here: 68.8 us
  Pallas kernels  68.1 us (99%)
  other arithmetic  0.72 us (1%)
    pallas_call x1, Pallas kernels, per_device(): pl.pallas_call(functools.partial(step_kernel, float(nodes * lax.axis_size...  68.1 us

profile of v8, /device:TPU:6, one launch (start us, length us, event | category | flops | bytes accessed | tf_op | source)
XLA Modules:
  0.0 68.8 jit_solution(9479703889538376223)
XLA Ops:
  0.0 68.1 %step.1 = bf16[16,4608]{1,0:T(8,128)(2,1)S(1)} custom-call(f32[16,4116]{1,0:T(8,128)} %psi_hbm.1, bf16[12,512,512]{2,1,0:T(8,128)(2,1)} %ham_hbm.1, s32[12,512]{1,0:T(8,128)} %conn_hbm.1, s32[588]{0:T(1024)} %face_hbm.1), custom_call_target="tpu_custom_call" | custom-call | tf_op jit(solution)/shard_map/step/pallas_call | solution.py:551
  68.1 0.7 %slice_convert_fusion = f32[16,4116]{1,0:T(8,128)} fusion(bf16[16,4608]{1,0:T(8,128)(2,1)S(1)} %step.1), kind=kLoop, calls=%fused_computation | loop fusion | flops 65856 | bytes 395136 | tf_op jit(solution)/shard_map/convert_element_type | solution.py:609

commit v9 on v7

--- a/solution.py
+++ b/solution.py
@@ -87,7 +87,7 @@
         return jnp.broadcast_to(value[:, j:j + 1], (step, 128))
 
     def spread_row(value, i):
-        return jnp.broadcast_to(value[i:i + 1, :], (step, 128))
+        return jnp.take_along_axis(value, jnp.full((step, 128), i, jnp.int32), axis=0)
 
     for number, top in enumerate(tops):
         if number > 0:
@@ -516,7 +516,7 @@
             def _():
                 keep(k).start()
 
-    tops = list(range(0, count, 2 * bands)) + [count - bands]
+    tops = [0, 4 * bands, 8 * bands, 10 * bands]
     factor_inverse(mat, tops, rows_of, deliver)
     rows_of(tops[-1], count)
     deliver(tops[-1], count)

time: 70 us -> 68.9 us (0.984)
  Pallas kernels: 69 us -> 67.9 us
    pallas_call x1, Pallas kernels: 69 us -> 67.9 us  [per_device(): pl.pallas_call(functools.partial(step_kernel, float(nodes * lax.axis_size...]
where the time goes in v9:
time: 68.9 us; the launch traced here: 68.6 us
  Pallas kernels  67.9 us (99%)
  other arithmetic  0.72 us (1%)
    pallas_call x1, Pallas kernels, per_device(): pl.pallas_call(functools.partial(step_kernel, float(nodes * lax.axis_size...  67.9 us

profile of v9, /device:TPU:6, one launch (start us, length us, event | category | flops | bytes accessed | tf_op | source)
XLA Modules:
  0.0 68.6 jit_solution(13382408935055618714)
XLA Ops:
  0.0 67.9 %step.1 = bf16[16,4608]{1,0:T(8,128)(2,1)S(1)} custom-call(f32[16,4116]{1,0:T(8,128)} %psi_hbm.1, bf16[12,512,512]{2,1,0:T(8,128)(2,1)} %ham_hbm.1, s32[12,512]{1,0:T(8,128)} %conn_hbm.1, s32[588]{0:T(1024)} %face_hbm.1), custom_call_target="tpu_custom_call" | custom-call | tf_op jit(solution)/shard_map/step/pallas_call | solution.py:551
  67.9 0.7 %slice_convert_fusion = f32[16,4116]{1,0:T(8,128)} fusion(bf16[16,4608]{1,0:T(8,128)(2,1)S(1)} %step.1), kind=kLoop, calls=%fused_computation | loop fusion | flops 65856 | bytes 395136 | tf_op jit(solution)/shard_map/convert_element_type | solution.py:609
